TPU v7x, 1024 devices: a whole 4x8x16 slice. The times are simulated.
1024 devices in a mesh: row: 64 (over y, z_hi, core), col: 16 (over x, z_lo).
Axes of the slice: x: 4, y: 8, z: 16 (z_hi: 4, z_lo: 4; z = z_hi * 4 + z_lo), core: 2. Of those that a mesh axis runs over, the one named last changes fastest.
Arguments:
- flow: float32 [2, 8, 512, 4096], P(None, None, 'row', 'col'), may hold values from -4 to 4
- temp: float32 [8, 512, 4096], P(None, 'row', 'col'), may hold values from -4 to 4
- tracers: float32 [64, 16, 8, 16, 2048], P('row', None, None, None, 'col'), may hold values from -4 to 4
- bottom: int32 [512, 4096], P('row', 'col'), may hold values from 0 to 8
- sunlight: float32 [512, 4096], P('row', 'col'), may hold values from 0.5 to 2
- rates: float32 [16, 16], replicated, may hold values from -2 to 2
Outputs:
- flow_out: float32 [2, 8, 512, 4096], P(None, None, 'row', 'col')
- temp_out: float32 [8, 512, 4096], P(None, 'row', 'col')
- tracers_out: float32 [64, 16, 8, 16, 2048], P('row', None, None, None, 'col')
Inputs may be any that keep to these rules, and one draw needn't show every extreme that they name: Columns are water at levels 0 to bottom - 1; 0 marks land.
All inputs are finite; a program needn't handle non-finite values.
Results may differ from a plain program's by a relative error of at most 0.0001.
Values sent between devices are 32-bit elements; how exact they have to be, the bound alone decides.
A program may use at most 32 MiB of HBM per device.

v0:
```python
import jax
import jax.numpy as jnp
from jax import lax
from jax.sharding import PartitionSpec as P

NZ = 8
KL = 4
STEPS = 2


time_step = 0.2
viscosity = 0.2
expansion = 0.05
coriolis_base = 0.5
kappa_base = 0.05
kappa_shear = 0.2
react_step = 0.25
water_absorb = 0.1
pigment_absorb = 0.6
heat_gain = 1.0


def extended(block, sides, width):
    for axis, dim in sides:
        count = lax.axis_size(axis)
        forward = [(i, i + 1) for i in range(count - 1)]
        backward = [(target, source) for source, target in forward]
        low = lax.ppermute(
            lax.slice_in_dim(block, block.shape[dim] - width, None, axis=dim), axis, forward
        )
        high = lax.ppermute(lax.slice_in_dim(block, 0, width, axis=dim), axis, backward)
        block = jnp.concatenate([low, block, high], axis=dim)
    return block


def from_partner(array, axis, bit):
    return lax.ppermute(array, axis, [(i, i ^ 1 << bit) for i in range(lax.axis_size(axis))])


def passed_along(array, axis, by):
    size = lax.axis_size(axis)
    pairs = [(i, i + by) for i in range(size) if 0 <= i + by < size]
    return lax.ppermute(array, axis, pairs)


def neighbour_sides(padded):
    middle = padded[..., 1:-1, 1:-1]
    return (
        middle,
        padded[..., 1:-1, 2:],
        padded[..., 1:-1, :-2],
        padded[..., 2:, 1:-1],
        padded[..., :-2, 1:-1],
    )


def shear_kappa(flow_u, flow_v):
    below_u = jnp.concatenate([flow_u[1:], flow_u[-1:]], axis=0)
    below_v = jnp.concatenate([flow_v[1:], flow_v[-1:]], axis=0)
    shear_sq = (flow_u - below_u) ** 2 + (flow_v - below_v) ** 2
    return kappa_base + kappa_shear * shear_sq / (1.0 + shear_sq)


def make_faces(padded):
    kappa_pad = shear_kappa(padded[0], padded[1])
    u_mid, u_east, u_west, u_north, u_south = neighbour_sides(padded[0])
    v_mid, v_east, v_west, v_north, v_south = neighbour_sides(padded[1])
    m_mid, m_east, m_west, m_north, m_south = neighbour_sides(padded[3])
    k_mid, k_east, k_west, k_north, k_south = neighbour_sides(kappa_pad)
    open_e = m_mid * m_east
    open_w = m_mid * m_west
    open_n = m_mid * m_north
    open_s = m_mid * m_south
    return jnp.stack(
        [
            0.5 * (u_mid + u_east) * open_e,
            0.5 * (u_mid + u_west) * open_w,
            0.5 * (v_mid + v_north) * open_n,
            0.5 * (v_mid + v_south) * open_s,
            0.5 * (k_mid + k_east) * open_e,
            0.5 * (k_mid + k_west) * open_w,
            0.5 * (k_mid + k_north) * open_n,
            0.5 * (k_mid + k_south) * open_s,
            m_mid,
        ]
    )


def transport(face_terms, padded):
    east_flux, west_flux, north_flux, south_flux = (
        face_terms[0],
        face_terms[1],
        face_terms[2],
        face_terms[3],
    )
    east_cond, west_cond, north_cond, south_cond = (
        face_terms[4],
        face_terms[5],
        face_terms[6],
        face_terms[7],
    )
    wet_mask = face_terms[8]
    middle, eastward, westward, northward, southward = neighbour_sides(padded)
    divergence = east_flux - west_flux + north_flux - south_flux
    upward = -lax.cumsum(divergence, axis=0, reverse=True)
    zero_top = jnp.zeros_like(upward[:1])
    w_bottom = jnp.concatenate([upward[1:], zero_top], axis=0)
    w_top = jnp.concatenate([zero_top, upward[1:]], axis=0)
    above_val = jnp.concatenate([middle[..., :1, :, :], middle[..., :-1, :, :]], axis=-3)
    below_val = jnp.concatenate([middle[..., 1:, :, :], middle[..., -1:, :, :]], axis=-3)
    advection = (
        east_flux * 0.5 * (middle + eastward)
        - west_flux * 0.5 * (middle + westward)
        + north_flux * 0.5 * (middle + northward)
        - south_flux * 0.5 * (middle + southward)
        + w_top * 0.5 * (middle + above_val)
        - w_bottom * 0.5 * (middle + below_val)
    )
    diffusion = (
        east_cond * (eastward - middle)
        + west_cond * (westward - middle)
        + north_cond * (northward - middle)
        + south_cond * (southward - middle)
    )
    return wet_mask * (middle + time_step * (diffusion - advection))


def momentum(padded, coriolis):
    pressure = -expansion * jnp.cumsum(padded[2], axis=0)
    p_mid, p_east, p_west, p_north, p_south = neighbour_sides(pressure)
    u_mid, u_east, u_west, u_north, u_south = neighbour_sides(padded[0])
    v_mid, v_east, v_west, v_north, v_south = neighbour_sides(padded[1])
    m_mid, m_east, m_west, m_north, m_south = neighbour_sides(padded[3])
    lap_u = m_mid * (
        m_east * (u_east - u_mid)
        + m_west * (u_west - u_mid)
        + m_north * (u_north - u_mid)
        + m_south * (u_south - u_mid)
    )
    lap_v = m_mid * (
        m_east * (v_east - v_mid)
        + m_west * (v_west - v_mid)
        + m_north * (v_north - v_mid)
        + m_south * (v_south - v_mid)
    )
    new_u = m_mid * (
        u_mid + time_step * (coriolis * v_mid - 0.5 * (p_east - p_west) + viscosity * lap_u)
    )
    new_v = m_mid * (
        v_mid + time_step * (-coriolis * u_mid - 0.5 * (p_north - p_south) + viscosity * lap_v)
    )
    return (new_u, new_v)


def absorption(pigment_top):
    squared = pigment_top * pigment_top
    transmit = jnp.exp(-(water_absorb + pigment_absorb * squared / (1.0 + squared)))
    above_light = jnp.cumprod(
        jnp.concatenate([jnp.ones_like(transmit[:1]), transmit[:-1]], axis=0), axis=0
    )
    return above_light * (1.0 - transmit)


def reaction(moved_field, rates, wet_mask):
    saturated = moved_field / jnp.sqrt(1.0 + moved_field * moved_field)
    coupling = jnp.einsum("nm,mkji->nkji", rates, saturated, precision=lax.Precision.HIGHEST)
    return moved_field + react_step * wet_mask * coupling


def split_lon(field, lower):
    half = field.shape[-1] // 2
    first, second = (field[..., :half], field[..., half:])
    return (jnp.where(lower, first, second), jnp.where(lower, second, first))


def split_lat(field, lower):
    half = field.shape[-2] // 2
    first, second = (field[..., :half, :], field[..., half:, :])
    return (jnp.where(lower, first, second), jnp.where(lower, second, first))


def join_lat(own_part, other_part, lower):
    return jnp.where(
        lower,
        jnp.concatenate([own_part, other_part], axis=-2),
        jnp.concatenate([other_part, own_part], axis=-2),
    )


def join_lon(own_part, other_part, lower):
    return jnp.where(
        lower,
        jnp.concatenate([own_part, other_part], axis=-1),
        jnp.concatenate([other_part, own_part], axis=-1),
    )


def ocean_step(flow_u, flow_v, heat_field, wet_mask, coriolis):
    padded = extended(
        jnp.stack([flow_u, flow_v, heat_field, wet_mask]), (("row", 2), ("col", 3)), 1
    )
    face_terms = make_faces(padded)
    new_u, new_v = momentum(padded, coriolis)
    return (face_terms, new_u, new_v, transport(face_terms, padded[2]))


def on_device(flow, temp, tracers, bottom, sunlight, rates):
    lat_dev = bottom.shape[0]
    lon_dev = bottom.shape[1]
    levels = lax.broadcasted_iota(jnp.int32, (NZ, lat_dev, lon_dev), 0)
    wet_mask = (levels < bottom[None]).astype(jnp.float32)
    row_index = lax.axis_index("row")
    lower = row_index % 2 == 0
    first_row = row_index * lat_dev
    latitude = (first_row + lax.broadcasted_iota(jnp.int32, (lat_dev, 1), 0)).astype(jnp.float32)
    total_lat = lat_dev * lax.axis_size("row")
    coriolis = coriolis_base * (2.0 * (latitude + 0.5) / total_lat - 1.0)
    flow_u = flow[0] * wet_mask
    flow_v = flow[1] * wet_mask
    heat_field = temp * wet_mask
    tracer_field = tracers[0]
    for step_index in range(STEPS):
        face_terms, flow_u, flow_v, heat_field = ocean_step(
            flow_u, flow_v, heat_field, wet_mask, coriolis
        )
        keep_faces, send_faces = split_lon(face_terms, lower)
        got_faces, got_east, got_west = from_partner(
            (send_faces, tracer_field[..., -1], tracer_field[..., 0]), "row", 0
        )
        block_faces = join_lat(keep_faces, got_faces, lower)
        if step_index == 0:
            tracer_field = tracer_field * block_faces[8]
        moved_cols = []
        for offset, column in ((1, got_east), (-1, got_west)):
            moved_cols.append(passed_along(column, "col", offset))
        west_rim = jnp.where(lower, moved_cols[0], got_east)
        east_rim = jnp.where(lower, got_west, moved_cols[1])
        moved_rows = []
        for offset, slab in ((2, tracer_field[..., -1:, :]), (-2, tracer_field[..., :1, :])):
            moved_rows.append(passed_along(slab, "row", offset))
        inner = jnp.concatenate([west_rim[..., None], tracer_field, east_rim[..., None]], axis=-1)
        widths = ((0, 0), (0, 0), (0, 0), (1, 1))
        padded = jnp.concatenate(
            [jnp.pad(moved_rows[0], widths), inner, jnp.pad(moved_rows[1], widths)], axis=-2
        )
        tracer_field = reaction(transport(block_faces, padded), rates, block_faces[8])
        profile = absorption(tracer_field[0, :KL])
        keep_light, send_light = split_lat(profile, lower)
        got_light = from_partner(send_light, "row", 0)
        returned = join_lon(keep_light, got_light, lower)
        heat_field = heat_field.at[:KL].add(heat_gain * sunlight * wet_mask[:KL] * returned)
    return (jnp.stack([flow_u, flow_v]), heat_field, tracer_field[None])


def solution(mesh):
    in_specs = (
        P(None, None, "row", "col"),
        P(None, "row", "col"),
        P("row", None, None, None, "col"),
        P("row", "col"),
        P("row", "col"),
        P(),
    )
    out_specs = (
        P(None, None, "row", "col"),
        P(None, "row", "col"),
        P("row", None, None, None, "col"),
    )
    return jax.shard_map(
        on_device, mesh=mesh, in_specs=in_specs, out_specs=out_specs, check_vma=False
    )
```

profile of v0, /device:TPU:33, one launch (start us, length us, event | category | flops | bytes accessed | tf_op | source)
XLA Modules:
  0.0 164.4 jit_solution(10320647088907947007)
XLA Ops:
  0.7 2.5 %slice_reduce_fusion.3 = (f32[16,8,16]{2,1,0:T(8,128)S(1)}, f32[16,8,16]{2,1,0:T(8,128)S(1)}) fusion(f32[16,8,16,128]{3,2,1,0:T(8,128)} %bitcast.171), kind=kLoop, calls=%fused_computation.71 | loop fusion | bytes 32768 | tf_op jit(solution)/shard_map/slice | solution.py:228
  3.2 2.7 %collective-permute-start.5 = (f32[16,8,16]{2,1,0:T(8,128)S(1)}, f32[16,8,16]{2,1,0:T(8,128)S(1)}, u32[]{:S(2)}, u32[]{:S(2)}) collective-permute-start(f32[16,8,16]{2,1,0:T(8,128)S(1)} %get-tuple-element.56), channel_id=1, source_target_pairs={{0,16},{16,0},{32,48},{48,32},{64,80},{80,64},{96,112},{112,96},{1... | collective-permute-start | bytes 24584 | tf_op jit(solution)/shard_map/ppermute | solution.py:37
  5.9 1.9 %collective-permute-start.7 = (f32[16,8,16]{2,1,0:T(8,128)S(1)}, f32[16,8,16]{2,1,0:T(8,128)S(1)}, u32[]{:S(2)}, u32[]{:S(2)}) collective-permute-start(f32[16,8,16]{2,1,0:T(8,128)S(1)} %get-tuple-element.57), channel_id=1, source_target_pairs={{0,16},{16,0},{32,48},{48,32},{64,80},{80,64},{96,112},{112,96},{1... | collective-permute-start | bytes 24584 | tf_op jit(solution)/shard_map/ppermute | solution.py:37
  8.0 11.0 %collective-permute-start = (f32[4,8,1,256]{3,2,1,0:T(1,128)S(1)}, f32[4,8,1,256]{3,2,1,0:T(1,128)S(1)}, u32[]{:S(2)}, u32[]{:S(2)}) collective-permute-start(f32[4,8,1,256]{3,2,1,0:T(1,128)S(1)} %get-tuple-element.152), channel_id=1, source_target_pairs={{0,16},{16,32},{32,48},{48,64},{64,80},{80,96},{96,112},{112,128},... | collective-permute-start | bytes 98312 | tf_op jit(solution)/shard_map/ppermute | solution.py:28
  19.0 1.9 %collective-permute-start.1 = (f32[4,8,1,256]{3,2,1,0:T(1,128)S(1)}, f32[4,8,1,256]{3,2,1,0:T(1,128)S(1)}, u32[]{:S(2)}, u32[]{:S(2)}) collective-permute-start(f32[4,8,1,256]{3,2,1,0:T(1,128)S(1)} %get-tuple-element.153), channel_id=1, source_target_pairs={{16,0},{32,16},{48,32},{64,48},{80,64},{96,80},{112,96},{128,112},... | collective-permute-start | bytes 98312 | tf_op jit(solution)/shard_map/ppermute | solution.py:31
  20.9 0.6 iota_compare_fusion
  21.5 1.3 collective-permute-start.6
  22.9 4.6 %collective-permute-start.8 = (f32[16,8,16]{2,1,0:T(8,128)S(1)}, f32[16,8,16]{2,1,0:T(8,128)S(1)}, u32[]{:S(2)}, u32[]{:S(2)}) collective-permute-start(f32[16,8,16]{2,1,0:T(8,128)S(1)} %collective-permute-done.7), channel_id=1, source_target_pairs={{0,1},{1,2},{2,3},{3,4},{4,5},{5,6},{6,7},{7,8},{8,9},{9,10},{10,1... | collective-permute-start | bytes 24584 | tf_op jit(solution)/shard_map/ppermute | solution.py:43
  27.6 0.6 collective-permute-done.1
  28.2 0.8 fusion.208
  29.1 4.0 %collective-permute-start.2 = (f32[4,8,10,1]{3,2,1,0:T(8,128)}, f32[4,8,10,1]{3,2,1,0:T(8,128)S(1)}, u32[]{:S(2)}, u32[]{:S(2)}) collective-permute-start(f32[4,8,10,1]{3,2,1,0:T(8,128)} %get-tuple-element.148), channel_id=1, source_target_pairs={{0,1},{1,2},{2,3},{3,4},{4,5},{5,6},{6,7},{7,8},{8,9},{9,10},{10,1... | collective-permute-start | bytes 3848 | tf_op jit(solution)/shard_map/ppermute | solution.py:28
  33.1 1.3 collective-permute-start.3
  34.4 0.8 copy.220
  35.2 0.8 copy.219
  36.1 1.3 collective-permute-done.2
  37.4 7.6 %collective-permute-done.3 = f32[4,8,10,1]{3,2,1,0:T(8,128)S(1)} collective-permute-done((f32[4,8,10,1]{3,2,1,0:T(8,128)S(1)}, f32[4,8,10,1]{3,2,1,0:T(8,128)S(1)}, u32[]{:S(2)}, u32[]{:S(2)}) %collective-permute-start.3) | collective-permute-done | bytes 1312 | tf_op jit(solution)/shard_map/ppermute | solution.py:31
  45.0 0.6 fusion.55
  47.4 7.6 %collective-permute-start.4 = (f32[9,8,8,128]{3,2,1,0:T(8,128)S(1)}, f32[9,8,8,128]{3,2,1,0:T(8,128)S(1)}, u32[]{:S(2)}, u32[]{:S(2)}) collective-permute-start(f32[9,8,8,128]{3,2,1,0:T(8,128)S(1)} %get-tuple-element.145), channel_id=1, source_target_pairs={{0,16},{16,0},{32,48},{48,32},{64,80},{80,64},{96,112},{112,96},{1... | collective-permute-start | bytes 884744 | tf_op jit(solution)/shard_map/ppermute | solution.py:37
  55.2 0.3 fusion.123
  55.7 0.4 collective-permute-done.4
  56.3 1.1 copy-done.1
  57.8 9.2 %collective-permute-start.9 = (f32[16,8,1,128]{3,2,1,0:T(1,128)S(1)}, f32[16,8,1,128]{3,2,1,0:T(1,128)S(1)}, u32[]{:S(2)}, u32[]{:S(2)}) collective-permute-start(f32[16,8,1,128]{3,2,1,0:T(1,128)S(1)} %get-tuple-element.100), channel_id=1, source_target_pairs={{32,0},{48,16},{64,32},{80,48},{96,64},{112,80},{128,96},{144,112}... | collective-permute-start | bytes 196616 | tf_op jit(solution)/shard_map/ppermute | solution.py:43
  67.0 1.9 %collective-permute-start.10 = (f32[16,8,1,128]{3,2,1,0:T(1,128)S(1)}, f32[16,8,1,128]{3,2,1,0:T(1,128)S(1)}, u32[]{:S(2)}, u32[]{:S(2)}) collective-permute-start(f32[16,8,1,128]{3,2,1,0:T(1,128)S(1)} %get-tuple-element.101), channel_id=1, source_target_pairs={{0,32},{16,48},{32,64},{48,80},{64,96},{80,112},{96,128},{112,144}... | collective-permute-start | bytes 196616 | tf_op jit(solution)/shard_map/ppermute | solution.py:43
  69.0 3.9 %collective-permute-done.9 = f32[16,8,1,128]{3,2,1,0:T(1,128)S(1)} collective-permute-done((f32[16,8,1,128]{3,2,1,0:T(1,128)S(1)}, f32[16,8,1,128]{3,2,1,0:T(1,128)S(1)}, u32[]{:S(2)}, u32[]{:S(2)}) %collective-permute-start.9) | collective-permute-done | bytes 65568 | tf_op jit(solution)/shard_map/ppermute | solution.py:43
  72.9 7.6 %collective-permute-done.10 = f32[16,8,1,128]{3,2,1,0:T(1,128)S(1)} collective-permute-done((f32[16,8,1,128]{3,2,1,0:T(1,128)S(1)}, f32[16,8,1,128]{3,2,1,0:T(1,128)S(1)}, u32[]{:S(2)}, u32[]{:S(2)}) %collective-permute-start.10) | collective-permute-done | bytes 65568 | tf_op jit(solution)/shard_map/ppermute | solution.py:43
  80.5 2.5 %rsqrt_multiply_fusion.1 = (f32[16,8,16,128]{3,2,1,0:T(8,128)S(1)}, f32[16,8,16,128]{3,2,1,0:T(8,128)S(1)}) fusion(f32[16,8,16,128]{3,2,1,0:T(8,128)S(1)} %broadcast_multiply_fusion, f32[16,1,16,128]{3,2,1,0:T(8,128)S(1)} %get-tuple-element.103, f32[16,7,16,128]{3,2,1,0:T(8,128)S(1)} %get-tuple-element.105, f32[8,16,128]{2,1,0:T(8,128)S(1)} %get-tuple-element.167, ...), kind=kLoop, calls=%fused_computation.89 | loop fusion | flops 13369344 | bytes 6111232 | tf_op jit(solution)/shard_map/div | solution.py:165
  83.1 1.6 fusion.50
  84.7 0.4 bitcast_add_fusion.1
  85.1 0.7 fusion.201
  85.8 0.9 slice_reduce_fusion.1
  86.7 1.4 fusion.203
  88.1 2.4 %collective-permute-start.11 = (f32[4,8,128]{2,1,0:T(8,128)S(1)}, f32[4,8,128]{2,1,0:T(8,128)S(1)}, u32[]{:S(2)}, u32[]{:S(2)}) collective-permute-start(f32[4,8,128]{2,1,0:T(8,128)S(1)} %get-tuple-element.171), channel_id=1, source_target_pairs={{0,16},{16,0},{32,48},{48,32},{64,80},{80,64},{96,112},{112,96},{1... | collective-permute-start | bytes 49160 | tf_op jit(solution)/shard_map/ppermute | solution.py:37
  90.6 1.9 %collective-permute-start.17 = (f32[16,8,16]{2,1,0:T(8,128)S(1)}, f32[16,8,16]{2,1,0:T(8,128)S(1)}, u32[]{:S(2)}, u32[]{:S(2)}) collective-permute-start(f32[16,8,16]{2,1,0:T(8,128)S(1)} %get-tuple-element.54), channel_id=1, source_target_pairs={{0,16},{16,0},{32,48},{48,32},{64,80},{80,64},{96,112},{112,96},{1... | collective-permute-start | bytes 24584 | tf_op jit(solution)/shard_map/ppermute | solution.py:37
  92.5 2.4 %collective-permute-start.19 = (f32[16,8,16]{2,1,0:T(8,128)S(1)}, f32[16,8,16]{2,1,0:T(8,128)S(1)}, u32[]{:S(2)}, u32[]{:S(2)}) collective-permute-start(f32[16,8,16]{2,1,0:T(8,128)S(1)} %get-tuple-element.55), channel_id=1, source_target_pairs={{0,16},{16,0},{32,48},{48,32},{64,80},{80,64},{96,112},{112,96},{1... | collective-permute-start | bytes 24584 | tf_op jit(solution)/shard_map/ppermute | solution.py:37
  94.9 0.7 fusion.202
  95.6 2.6 %collective-permute-start.21 = (f32[16,8,1,128]{3,2,1,0:T(1,128)}, f32[16,8,1,128]{3,2,1,0:T(1,128)}, u32[]{:S(2)}, u32[]{:S(2)}) collective-permute-start(f32[16,8,1,128]{3,2,1,0:T(1,128)} %get-tuple-element.94), channel_id=1, source_target_pairs={{32,0},{48,16},{64,32},{80,48},{96,64},{112,80},{128,96},{144,112}... | collective-permute-start | bytes 196616 | tf_op jit(solution)/shard_map/ppermute | solution.py:43
  98.3 6.5 %collective-permute-start.22 = (f32[16,8,1,128]{3,2,1,0:T(1,128)}, f32[16,8,1,128]{3,2,1,0:T(1,128)}, u32[]{:S(2)}, u32[]{:S(2)}) collective-permute-start(f32[16,8,1,128]{3,2,1,0:T(1,128)} %get-tuple-element.95), channel_id=1, source_target_pairs={{0,32},{16,48},{32,64},{48,80},{64,96},{80,112},{96,128},{112,144}... | collective-permute-start | bytes 196616 | tf_op jit(solution)/shard_map/ppermute | solution.py:43
  104.8 1.3 collective-permute-start.18
  106.1 4.7 %collective-permute-start.20 = (f32[16,8,16]{2,1,0:T(8,128)S(1)}, f32[16,8,16]{2,1,0:T(8,128)S(1)}, u32[]{:S(2)}, u32[]{:S(2)}) collective-permute-start(f32[16,8,16]{2,1,0:T(8,128)S(1)} %collective-permute-done.19), channel_id=1, source_target_pairs={{0,1},{1,2},{2,3},{3,4},{4,5},{5,6},{6,7},{7,8},{8,9},{9,10},{10,1... | collective-permute-start | bytes 24584 | tf_op jit(solution)/shard_map/ppermute | solution.py:43
  111.0 2.4 %collective-permute-start.12 = (f32[4,8,1,256]{3,2,1,0:T(1,128)S(1)}, f32[4,8,1,256]{3,2,1,0:T(1,128)S(1)}, u32[]{:S(2)}, u32[]{:S(2)}) collective-permute-start(f32[4,8,1,256]{3,2,1,0:T(1,128)S(1)} %get-tuple-element.150), channel_id=1, source_target_pairs={{0,16},{16,32},{32,48},{48,64},{64,80},{80,96},{96,112},{112,128},... | collective-permute-start | bytes 98312 | tf_op jit(solution)/shard_map/ppermute | solution.py:28
  113.4 2.3 %collective-permute-start.13 = (f32[4,8,1,256]{3,2,1,0:T(1,128)S(1)}, f32[4,8,1,256]{3,2,1,0:T(1,128)S(1)}, u32[]{:S(2)}, u32[]{:S(2)}) collective-permute-start(f32[4,8,1,256]{3,2,1,0:T(1,128)S(1)} %get-tuple-element.151), channel_id=1, source_target_pairs={{16,0},{32,16},{48,32},{64,48},{80,64},{96,80},{112,96},{128,112},... | collective-permute-start | bytes 98312 | tf_op jit(solution)/shard_map/ppermute | solution.py:31
  115.7 0.6 select_bitcast_fusion.1
  116.4 6.4 %collective-permute-done.13 = f32[4,8,1,256]{3,2,1,0:T(1,128)S(1)} collective-permute-done((f32[4,8,1,256]{3,2,1,0:T(1,128)S(1)}, f32[4,8,1,256]{3,2,1,0:T(1,128)S(1)}, u32[]{:S(2)}, u32[]{:S(2)}) %collective-permute-start.13) | collective-permute-done | bytes 32800 | tf_op jit(solution)/shard_map/ppermute | solution.py:31
  122.8 0.5 copy-done.10
  123.3 0.9 fusion.207
  124.2 4.9 %collective-permute-start.14 = (f32[4,8,10,1]{3,2,1,0:T(8,128)}, f32[4,8,10,1]{3,2,1,0:T(8,128)}, u32[]{:S(2)}, u32[]{:S(2)}) collective-permute-start(f32[4,8,10,1]{3,2,1,0:T(8,128)} %get-tuple-element.146), channel_id=1, source_target_pairs={{0,1},{1,2},{2,3},{3,4},{4,5},{5,6},{6,7},{7,8},{8,9},{9,10},{10,1... | collective-permute-start | bytes 3848 | tf_op jit(solution)/shard_map/ppermute | solution.py:28
  129.1 1.5 collective-permute-start.15
  130.6 0.8 copy.226
  131.4 1.7 %copy.225 = f32[16,8,16,1]{3,2,1,0:T(8,128)S(1)} copy(f32[16,8,16,1]{2,1,0,3:T(8,128)} %select_bitcast_fusion.1) | data formatting | bytes 16384 | tf_op jit(solution)/shard_map/broadcast_in_dim | solution.py:241
  133.1 11.9 %collective-permute-done.15 = f32[4,8,10,1]{3,2,1,0:T(8,128)} collective-permute-done((f32[4,8,10,1]{3,2,1,0:T(8,128)}, f32[4,8,10,1]{3,2,1,0:T(8,128)}, u32[]{:S(2)}, u32[]{:S(2)}) %collective-permute-start.15) | collective-permute-done | bytes 1312 | tf_op jit(solution)/shard_map/ppermute | solution.py:31
  145.0 1.7 %fusion.59 = f32[4,8,10,258]{3,2,1,0:T(8,128)S(1)} fusion(f32[1,8,8,256]{3,2,1,0:T(8,128)S(1)} %fusion.174, f32[4,8,10,1]{3,2,1,0:T(8,128)} %collective-permute-done.15, f32[4,8,1,256]{3,2,1,0:T(1,128)} %copy-done.10, f32[1,8,8,256]{3,2,1,0:T(8,128)S(1)} %fusion.185, f32[1,8,8,256]{3,2,1,0:T(8,128)S(1)} %fusion.123, f32[1,8,8,256]{3,2,1,0:T(8,128)S(1)} %fusion.135, ...), kind=kLoop, calls=%fused_computation.97 | loop fusion | flops 577920 | bytes 660480 | tf_op jit(solution)/shard_map/concatenate | solution.py:32
  146.8 0.6 copy-done.18
  147.7 0.3 copy-done.16
  149.8 2.6 %collective-permute-start.16 = (f32[9,8,8,128]{3,2,1,0:T(8,128)S(1)}, f32[9,8,8,128]{3,2,1,0:T(8,128)S(1)}, u32[]{:S(2)}, u32[]{:S(2)}) collective-permute-start(f32[9,8,8,128]{3,2,1,0:T(8,128)S(1)} %get-tuple-element.133), channel_id=1, source_target_pairs={{0,16},{16,0},{32,48},{48,32},{64,80},{80,64},{96,112},{112,96},{1... | collective-permute-start | bytes 884744 | tf_op jit(solution)/shard_map/ppermute | solution.py:37
  152.7 0.9 collective-permute-done.16
  153.8 0.7 copy-done.5
  154.5 0.4 copy-done.2
  154.9 0.3 copy-done.3
  155.2 3.3 %rsqrt_multiply_fusion = (f32[16,8,16,128]{3,2,1,0:T(8,128)S(1)}, f32[16,8,16,128]{3,2,1,0:T(8,128)S(1)}) fusion(f32[16,8,16,128]{3,2,1,0:T(8,128)S(1)} %bitcast_add_fusion.1, f32[16,1,16,128]{3,2,1,0:T(8,128)S(1)} %copy-done.5, f32[16,7,16,128]{3,2,1,0:T(8,128)S(1)} %copy-done.3, f32[8,16,128]{2,1,0:T(8,128)S(1)} %get-tuple-element.165, ...), kind=kLoop, calls=%fused_computation.88 | loop fusion | flops 13369344 | bytes 6111232 | tf_op jit(solution)/shard_map/div | solution.py:165
  158.4 1.6 fusion.48
  160.1 0.4 bitcast_add_fusion
  160.5 2.4 %collective-permute-start.23 = (f32[4,8,128]{2,1,0:T(8,128)S(1)}, f32[4,8,128]{2,1,0:T(8,128)S(1)}, u32[]{:S(2)}, u32[]{:S(2)}) collective-permute-start(f32[4,8,128]{2,1,0:T(8,128)S(1)} %get-tuple-element.169), channel_id=1, source_target_pairs={{0,16},{16,0},{32,48},{48,32},{64,80},{80,64},{96,112},{112,96},{1... | collective-permute-start | bytes 49160 | tf_op jit(solution)/shard_map/ppermute | solution.py:37
  162.9 0.7 pad_maximum_fusion.18
  163.8 0.6 copy-done.6
  (124 shorter events, 5.9 us)
Async XLA Ops:
  0.6 82.4 %copy-start = (f32[16,16]{1,0:T(8,128)S(1)}, f32[16,16]{1,0:T(8,128)}, u32[]{:S(2)}) copy-start(f32[16,16]{1,0:T(8,128)} %param.15) | copy-start | bytes 3076
  0.6 7.2 %copy-start.7 = (s32[8,256]{1,0:T(8,128)S(1)}, s32[8,256]{1,0:T(8,128)}, u32[]{:S(2)}) copy-start(s32[8,256]{1,0:T(8,128)} %param.13) | copy-start | bytes 24580
  0.7 7.2 %copy-start.13 = (f32[8,8,256]{2,1,0:T(8,128)S(1)}, f32[8,8,256]{2,1,0:T(8,128)}, u32[]{:S(2)}) copy-start(f32[8,8,256]{2,1,0:T(8,128)} %param.11) | copy-start | bytes 196612
  3.2 4.7 %copy-start.8 = (f32[2,8,8,256]{3,2,1,0:T(8,128)S(1)}, f32[2,8,8,256]{3,2,1,0:T(8,128)}, u32[]{:S(2)}) copy-start(f32[2,8,8,256]{3,2,1,0:T(8,128)} %param.10) | copy-start | bytes 393220
  3.2 18.4 %collective-permute-start.5 = (f32[16,8,16]{2,1,0:T(8,128)S(1)}, f32[16,8,16]{2,1,0:T(8,128)S(1)}, u32[]{:S(2)}, u32[]{:S(2)}) collective-permute-start(f32[16,8,16]{2,1,0:T(8,128)S(1)} %get-tuple-element.56), channel_id=1, source_target_pairs={{0,16},{16,0},{32,48},{48,32},{64,80},{80,64},{96,112},{112,96},{1... | collective-permute-start | bytes 24584 | tf_op jit(solution)/shard_map/ppermute | solution.py:37
  5.9 17.0 %collective-permute-start.7 = (f32[16,8,16]{2,1,0:T(8,128)S(1)}, f32[16,8,16]{2,1,0:T(8,128)S(1)}, u32[]{:S(2)}, u32[]{:S(2)}) collective-permute-start(f32[16,8,16]{2,1,0:T(8,128)S(1)} %get-tuple-element.57), channel_id=1, source_target_pairs={{0,16},{16,0},{32,48},{48,32},{64,80},{80,64},{96,112},{112,96},{1... | collective-permute-start | bytes 24584 | tf_op jit(solution)/shard_map/ppermute | solution.py:37
  8.0 19.6 %collective-permute-start = (f32[4,8,1,256]{3,2,1,0:T(1,128)S(1)}, f32[4,8,1,256]{3,2,1,0:T(1,128)S(1)}, u32[]{:S(2)}, u32[]{:S(2)}) collective-permute-start(f32[4,8,1,256]{3,2,1,0:T(1,128)S(1)} %get-tuple-element.152), channel_id=1, source_target_pairs={{0,16},{16,32},{32,48},{48,64},{64,80},{80,96},{96,112},{112,128},... | collective-permute-start | bytes 98312 | tf_op jit(solution)/shard_map/ppermute | solution.py:28
  19.0 9.1 %collective-permute-start.1 = (f32[4,8,1,256]{3,2,1,0:T(1,128)S(1)}, f32[4,8,1,256]{3,2,1,0:T(1,128)S(1)}, u32[]{:S(2)}, u32[]{:S(2)}) collective-permute-start(f32[4,8,1,256]{3,2,1,0:T(1,128)S(1)} %get-tuple-element.153), channel_id=1, source_target_pairs={{16,0},{32,16},{48,32},{64,48},{80,64},{96,80},{112,96},{128,112},... | collective-permute-start | bytes 98312 | tf_op jit(solution)/shard_map/ppermute | solution.py:31
  21.5 6.0 %collective-permute-start.6 = (f32[16,8,16]{2,1,0:T(8,128)S(1)}, f32[16,8,16]{2,1,0:T(8,128)S(1)}, u32[]{:S(2)}, u32[]{:S(2)}) collective-permute-start(f32[16,8,16]{2,1,0:T(8,128)S(1)} %collective-permute-done.5), channel_id=1, source_target_pairs={{1,0},{2,1},{3,2},{4,3},{5,4},{6,5},{7,6},{8,7},{9,8},{10,9},{11,1... | collective-permute-start | bytes 24584 | tf_op jit(solution)/shard_map/ppermute | solution.py:43
  22.8 32.3 %copy-start.17 = (f32[8]{0:T(128)}, f32[8]{0:T(128)S(1)}, u32[]{:S(2)}) copy-start(f32[8]{0:T(128)S(1)} %get-tuple-element.173) | copy-start | bytes 100
  22.9 32.6 %copy-start.15 = (f32[8]{0:T(128)}, f32[8]{0:T(128)S(1)}, u32[]{:S(2)}) copy-start(f32[8]{0:T(128)S(1)} %get-tuple-element.172) | copy-start | bytes 100
  22.9 11.5 %collective-permute-start.8 = (f32[16,8,16]{2,1,0:T(8,128)S(1)}, f32[16,8,16]{2,1,0:T(8,128)S(1)}, u32[]{:S(2)}, u32[]{:S(2)}) collective-permute-start(f32[16,8,16]{2,1,0:T(8,128)S(1)} %collective-permute-done.7), channel_id=1, source_target_pairs={{0,1},{1,2},{2,3},{3,4},{4,5},{5,6},{6,7},{7,8},{8,9},{9,10},{10,1... | collective-permute-start | bytes 24584 | tf_op jit(solution)/shard_map/ppermute | solution.py:43
  29.1 8.3 %collective-permute-start.2 = (f32[4,8,10,1]{3,2,1,0:T(8,128)}, f32[4,8,10,1]{3,2,1,0:T(8,128)S(1)}, u32[]{:S(2)}, u32[]{:S(2)}) collective-permute-start(f32[4,8,10,1]{3,2,1,0:T(8,128)} %get-tuple-element.148), channel_id=1, source_target_pairs={{0,1},{1,2},{2,3},{3,4},{4,5},{5,6},{6,7},{7,8},{8,9},{9,10},{10,1... | collective-permute-start | bytes 3848 | tf_op jit(solution)/shard_map/ppermute | solution.py:28
  33.1 11.9 %collective-permute-start.3 = (f32[4,8,10,1]{3,2,1,0:T(8,128)S(1)}, f32[4,8,10,1]{3,2,1,0:T(8,128)S(1)}, u32[]{:S(2)}, u32[]{:S(2)}) collective-permute-start(f32[4,8,10,1]{3,2,1,0:T(8,128)S(1)} %get-tuple-element.149), channel_id=1, source_target_pairs={{1,0},{2,1},{3,2},{4,3},{5,4},{6,5},{7,6},{8,7},{9,8},{10,9},{11,1... | collective-permute-start | bytes 3848 | tf_op jit(solution)/shard_map/ppermute | solution.py:31
  47.4 8.8 %collective-permute-start.4 = (f32[9,8,8,128]{3,2,1,0:T(8,128)S(1)}, f32[9,8,8,128]{3,2,1,0:T(8,128)S(1)}, u32[]{:S(2)}, u32[]{:S(2)}) collective-permute-start(f32[9,8,8,128]{3,2,1,0:T(8,128)S(1)} %get-tuple-element.145), channel_id=1, source_target_pairs={{0,16},{16,0},{32,48},{48,32},{64,80},{80,64},{96,112},{112,96},{1... | collective-permute-start | bytes 884744 | tf_op jit(solution)/shard_map/ppermute | solution.py:37
  56.2 1.2 copy-start.1
  57.8 15.1 %collective-permute-start.9 = (f32[16,8,1,128]{3,2,1,0:T(1,128)S(1)}, f32[16,8,1,128]{3,2,1,0:T(1,128)S(1)}, u32[]{:S(2)}, u32[]{:S(2)}) collective-permute-start(f32[16,8,1,128]{3,2,1,0:T(1,128)S(1)} %get-tuple-element.100), channel_id=1, source_target_pairs={{32,0},{48,16},{64,32},{80,48},{96,64},{112,80},{128,96},{144,112}... | collective-permute-start | bytes 196616 | tf_op jit(solution)/shard_map/ppermute | solution.py:43
  67.0 13.5 %collective-permute-start.10 = (f32[16,8,1,128]{3,2,1,0:T(1,128)S(1)}, f32[16,8,1,128]{3,2,1,0:T(1,128)S(1)}, u32[]{:S(2)}, u32[]{:S(2)}) collective-permute-start(f32[16,8,1,128]{3,2,1,0:T(1,128)S(1)} %get-tuple-element.101), channel_id=1, source_target_pairs={{0,32},{16,48},{32,64},{48,80},{64,96},{80,112},{96,128},{112,144}... | collective-permute-start | bytes 196616 | tf_op jit(solution)/shard_map/ppermute | solution.py:43
  88.1 22.7 %collective-permute-start.11 = (f32[4,8,128]{2,1,0:T(8,128)S(1)}, f32[4,8,128]{2,1,0:T(8,128)S(1)}, u32[]{:S(2)}, u32[]{:S(2)}) collective-permute-start(f32[4,8,128]{2,1,0:T(8,128)S(1)} %get-tuple-element.171), channel_id=1, source_target_pairs={{0,16},{16,0},{32,48},{48,32},{64,80},{80,64},{96,112},{112,96},{1... | collective-permute-start | bytes 49160 | tf_op jit(solution)/shard_map/ppermute | solution.py:37
  90.6 14.2 %collective-permute-start.17 = (f32[16,8,16]{2,1,0:T(8,128)S(1)}, f32[16,8,16]{2,1,0:T(8,128)S(1)}, u32[]{:S(2)}, u32[]{:S(2)}) collective-permute-start(f32[16,8,16]{2,1,0:T(8,128)S(1)} %get-tuple-element.54), channel_id=1, source_target_pairs={{0,16},{16,0},{32,48},{48,32},{64,80},{80,64},{96,112},{112,96},{1... | collective-permute-start | bytes 24584 | tf_op jit(solution)/shard_map/ppermute | solution.py:37
  92.5 18.4 %copy-start.11 = (pred[8,8,256]{2,1,0:T(8,128)(4,1)S(1)}, pred[8,8,256]{2,1,0:T(8,128)(4,1)}, u32[]{:S(2)}) copy-start(pred[8,8,256]{2,1,0:T(8,128)(4,1)} %iota_compare_fusion) | copy-start | bytes 49156
  92.5 13.6 %collective-permute-start.19 = (f32[16,8,16]{2,1,0:T(8,128)S(1)}, f32[16,8,16]{2,1,0:T(8,128)S(1)}, u32[]{:S(2)}, u32[]{:S(2)}) collective-permute-start(f32[16,8,16]{2,1,0:T(8,128)S(1)} %get-tuple-element.55), channel_id=1, source_target_pairs={{0,16},{16,0},{32,48},{48,32},{64,80},{80,64},{96,112},{112,96},{1... | collective-permute-start | bytes 24584 | tf_op jit(solution)/shard_map/ppermute | solution.py:37
  94.9 16.0 %copy-start.14 = (f32[8,256]{1,0:T(8,128)S(1)}, f32[8,256]{1,0:T(8,128)}, u32[]{:S(2)}) copy-start(f32[8,256]{1,0:T(8,128)} %param.14) | copy-start | bytes 24580
  95.6 58.2 %collective-permute-start.21 = (f32[16,8,1,128]{3,2,1,0:T(1,128)}, f32[16,8,1,128]{3,2,1,0:T(1,128)}, u32[]{:S(2)}, u32[]{:S(2)}) collective-permute-start(f32[16,8,1,128]{3,2,1,0:T(1,128)} %get-tuple-element.94), channel_id=1, source_target_pairs={{32,0},{48,16},{64,32},{80,48},{96,64},{112,80},{128,96},{144,112}... | collective-permute-start | bytes 196616 | tf_op jit(solution)/shard_map/ppermute | solution.py:43
  98.3 55.6 %collective-permute-start.22 = (f32[16,8,1,128]{3,2,1,0:T(1,128)}, f32[16,8,1,128]{3,2,1,0:T(1,128)}, u32[]{:S(2)}, u32[]{:S(2)}) collective-permute-start(f32[16,8,1,128]{3,2,1,0:T(1,128)} %get-tuple-element.95), channel_id=1, source_target_pairs={{0,32},{16,48},{32,64},{48,80},{64,96},{80,112},{96,128},{112,144}... | collective-permute-start | bytes 196616 | tf_op jit(solution)/shard_map/ppermute | solution.py:43
  104.8 8.6 %collective-permute-start.18 = (f32[16,8,16]{2,1,0:T(8,128)S(1)}, f32[16,8,16]{2,1,0:T(8,128)S(1)}, u32[]{:S(2)}, u32[]{:S(2)}) collective-permute-start(f32[16,8,16]{2,1,0:T(8,128)S(1)} %collective-permute-done.17), channel_id=1, source_target_pairs={{1,0},{2,1},{3,2},{4,3},{5,4},{6,5},{7,6},{8,7},{9,8},{10,9},{11,1... | collective-permute-start | bytes 24584 | tf_op jit(solution)/shard_map/ppermute | solution.py:43
  106.1 24.4 %collective-permute-start.20 = (f32[16,8,16]{2,1,0:T(8,128)S(1)}, f32[16,8,16]{2,1,0:T(8,128)S(1)}, u32[]{:S(2)}, u32[]{:S(2)}) collective-permute-start(f32[16,8,16]{2,1,0:T(8,128)S(1)} %collective-permute-done.19), channel_id=1, source_target_pairs={{0,1},{1,2},{2,3},{3,4},{4,5},{5,6},{6,7},{7,8},{8,9},{9,10},{10,1... | collective-permute-start | bytes 24584 | tf_op jit(solution)/shard_map/ppermute | solution.py:43
  111.0 5.4 %collective-permute-start.12 = (f32[4,8,1,256]{3,2,1,0:T(1,128)S(1)}, f32[4,8,1,256]{3,2,1,0:T(1,128)S(1)}, u32[]{:S(2)}, u32[]{:S(2)}) collective-permute-start(f32[4,8,1,256]{3,2,1,0:T(1,128)S(1)} %get-tuple-element.150), channel_id=1, source_target_pairs={{0,16},{16,32},{32,48},{48,64},{64,80},{80,96},{96,112},{112,128},... | collective-permute-start | bytes 98312 | tf_op jit(solution)/shard_map/ppermute | solution.py:28
  113.4 9.3 %collective-permute-start.13 = (f32[4,8,1,256]{3,2,1,0:T(1,128)S(1)}, f32[4,8,1,256]{3,2,1,0:T(1,128)S(1)}, u32[]{:S(2)}, u32[]{:S(2)}) collective-permute-start(f32[4,8,1,256]{3,2,1,0:T(1,128)S(1)} %get-tuple-element.151), channel_id=1, source_target_pairs={{16,0},{32,16},{48,32},{64,48},{80,64},{96,80},{112,96},{128,112},... | collective-permute-start | bytes 98312 | tf_op jit(solution)/shard_map/ppermute | solution.py:31
  116.4 6.5 %copy-start.9 = (f32[4,8,1,256]{3,2,1,0:T(1,128)}, f32[4,8,1,256]{3,2,1,0:T(1,128)S(1)}, u32[]{:S(2)}) copy-start(f32[4,8,1,256]{3,2,1,0:T(1,128)S(1)} %collective-permute-done.12) | copy-start | bytes 98308
  122.7 0.6 copy-start.10
  124.2 8.9 %collective-permute-start.14 = (f32[4,8,10,1]{3,2,1,0:T(8,128)}, f32[4,8,10,1]{3,2,1,0:T(8,128)}, u32[]{:S(2)}, u32[]{:S(2)}) collective-permute-start(f32[4,8,10,1]{3,2,1,0:T(8,128)} %get-tuple-element.146), channel_id=1, source_target_pairs={{0,1},{1,2},{2,3},{3,4},{4,5},{5,6},{6,7},{7,8},{8,9},{9,10},{10,1... | collective-permute-start | bytes 3848 | tf_op jit(solution)/shard_map/ppermute | solution.py:28
  129.1 15.8 %collective-permute-start.15 = (f32[4,8,10,1]{3,2,1,0:T(8,128)}, f32[4,8,10,1]{3,2,1,0:T(8,128)}, u32[]{:S(2)}, u32[]{:S(2)}) collective-permute-start(f32[4,8,10,1]{3,2,1,0:T(8,128)} %get-tuple-element.147), channel_id=1, source_target_pairs={{1,0},{2,1},{3,2},{4,3},{5,4},{6,5},{7,6},{8,7},{9,8},{10,9},{11,1... | collective-permute-start | bytes 3848 | tf_op jit(solution)/shard_map/ppermute | solution.py:31
  146.8 0.6 copy-start.18
  147.4 0.6 copy-start.16
  149.8 3.8 %collective-permute-start.16 = (f32[9,8,8,128]{3,2,1,0:T(8,128)S(1)}, f32[9,8,8,128]{3,2,1,0:T(8,128)S(1)}, u32[]{:S(2)}, u32[]{:S(2)}) collective-permute-start(f32[9,8,8,128]{3,2,1,0:T(8,128)S(1)} %get-tuple-element.133), channel_id=1, source_target_pairs={{0,16},{16,0},{32,48},{48,32},{64,80},{80,64},{96,112},{112,96},{1... | collective-permute-start | bytes 884744 | tf_op jit(solution)/shard_map/ppermute | solution.py:37
  153.6 0.9 copy-start.5
  153.7 1.2 copy-start.2
  153.7 1.5 copy-start.3
  160.4 3.4 %copy-start.4 = (f32[16,8,16,128]{3,2,1,0:T(8,128)}, f32[16,8,16,128]{3,2,1,0:T(8,128)S(1)}, u32[]{:S(2)}) copy-start(f32[16,8,16,128]{3,2,1,0:T(8,128)S(1)} %bitcast_add_fusion) | copy-start | bytes 3145732
  160.5 3.2 %copy-start.12 = (pred[8,8,256]{2,1,0:T(8,128)(4,1)S(1)}, pred[8,8,256]{2,1,0:T(8,128)(4,1)}, u32[]{:S(2)}) copy-start(pred[8,8,256]{2,1,0:T(8,128)(4,1)} %iota_compare_fusion) | copy-start | bytes 49156
  160.5 3.2 %collective-permute-start.23 = (f32[4,8,128]{2,1,0:T(8,128)S(1)}, f32[4,8,128]{2,1,0:T(8,128)S(1)}, u32[]{:S(2)}, u32[]{:S(2)}) collective-permute-start(f32[4,8,128]{2,1,0:T(8,128)S(1)} %get-tuple-element.169), channel_id=1, source_target_pairs={{0,16},{16,0},{32,48},{48,32},{64,80},{80,64},{96,112},{112,96},{1... | collective-permute-start | bytes 49160 | tf_op jit(solution)/shard_map/ppermute | solution.py:37
  163.8 0.6 copy-start.6
where the time goes:
time: 165 us; the launch traced here: 164 us
  starting transfers between devices  85.5 us (52%)
  waiting for transfers between devices  40.9 us (25%)
  local copies, waits for them, and re-layouts  17.6 us (11%)
  other arithmetic  15.5 us (9%)
  matrix products  3.22 us (2%)
  between operations  1.72 us (1%)
    ppermute x8, starting transfers between devices, passed_along(): return lax.ppermute(array, axis, pairs)  32.2 us
    ppermute x4, waiting for transfers between devices, extended(): lax.ppermute(lax.slice_in_dim(block, 0, width, axis=dim), axis, backward)  26.4 us
    ppermute x8, starting transfers between devices, from_partner(): lax.ppermute(array, axis, [(i, i ^ 1 << bit) for i in range(lax.axis_size...  24 us
    ppermute x4, starting transfers between devices, extended(): lax.ppermute(lax.slice_in_dim(block, block.shape[dim] - width, None, axis...  22.3 us
    ppermute x8, waiting for transfers between devices, passed_along(): return lax.ppermute(array, axis, pairs)  11.6 us
    ppermute x4, starting transfers between devices, extended(): lax.ppermute(lax.slice_in_dim(block, 0, width, axis=dim), axis, backward)  6.98 us
    div x2, other arithmetic, reaction(): saturated = moved_field / jnp.sqrt(1.0 + moved_field * moved_field)  5.77 us
    unnamed x39, local copies, waits for them, and re-layouts  4.55 us
  transfers between devices with their start and end apart: 24, of which 10 were waited for; matrix products, arithmetic and copies ran while one was open for 8% of the time, Pallas kernels for 0%

commit v1 on v0

v1 whole, which is shorter than its diff:
```python
import functools

import jax
import jax.numpy as jnp
from jax import lax
from jax.experimental import pallas as pl
from jax.experimental.pallas import tpu as pltpu
from jax.sharding import PartitionSpec as P

MESH = pl.DeviceIdType.MESH
NT = 16
NZ = 8
KL = 4

time_step = 0.2
viscosity = 0.2
expansion = 0.05
coriolis_base = 0.5
kappa_base = 0.05
kappa_shear = 0.2
react_step = 0.25
water_absorb = 0.1
pigment_absorb = 0.6
heat_gain = 1.0


def kernel(
    n_row, n_col,
    flow, temp, tr, bot, sun, rates,
    flow_out, temp_out, tr_out,
    c0, c1, c2, p0, p1, psat, fm0, fp0, fm1, fp1, kpm, kpp, am, ap, ap_flow, wmat,
    xo, xw, xe, xc, pf, pt, pb, ps, fo, fr,
    send, recv,
):
    row = lax.axis_index("row")
    col = lax.axis_index("col")
    half = lax.rem(row, 2)
    chip = row // 2
    other = 2 * chip + 1 - half
    west_col = col - 1 + half
    east_col = col + half
    has_w = west_col >= 0
    has_e = east_col < n_col
    has_n = row + 2 < n_row
    has_s = row >= 2
    partner = (other, col)
    west = (other, west_col)
    east = (other, east_col)
    north = (row + 2, col)
    south = (row - 2, col)
    targets = (
        (has_n, north), (has_s, south), (has_e, east), (has_w, west),
        (has_n & has_e, (other + 2, east_col)), (has_n & has_w, (other + 2, west_col)),
        (has_s & has_e, (other - 2, east_col)), (has_s & has_w, (other - 2, west_col)),
    )

    barrier = pltpu.get_barrier_semaphore()
    count = jnp.int32(0)
    for here, target in targets:
        count = count + here.astype(jnp.int32)

        @pl.when(here)
        def _(target=target):
            pl.semaphore_signal(barrier, inc=1, device_id=target, device_id_type=MESH)

    lane = lax.broadcasted_iota(jnp.int32, (NZ, 128), 1)
    level = lax.broadcasted_iota(jnp.int32, (NZ, 128), 0)
    level_f = level.astype(jnp.float32)
    group = lax.rem(lane, 8)
    zero = jnp.zeros((NZ, 128), jnp.float32)

    def roll(x, by, axis=1):
        by = by % x.shape[axis]
        return pltpu.roll(x, by, axis) if by else x

    def turn_in(n, carry):
        for t in range(2):
            c0[pl.ds(2 + 8 * t, 8), n] = jnp.swapaxes(tr[0, n, :, 8 * t : 8 * t + 8, :], 0, 1)
        return carry

    lax.fori_loop(0, NT, turn_in, 0)

    pl.semaphore_wait(barrier, count)

    def copy(src, dst, k, target):
        return pltpu.make_async_remote_copy(
            src_ref=src, dst_ref=dst, send_sem=send.at[k], recv_sem=recv.at[k],
            device_id=target, device_id_type=MESH,
        )

    own_half = pl.ds(pl.multiple_of(half * 128, 128), 128)
    other_half = pl.ds(pl.multiple_of((1 - half) * 128, 128), 128)
    to_partner = (
        copy(flow.at[:, :, :, other_half], pf, 0, partner),
        copy(temp.at[:, :, other_half], pt, 1, partner),
        copy(bot.at[:, other_half], pb, 2, partner),
        copy(sun.at[:, other_half], ps, 3, partner),
    )
    near = (
        (copy(c0.at[17], c0.at[1], 4, north), has_n, has_s),
        (copy(c0.at[2], c0.at[18], 5, south), has_s, has_n),
    )
    far = (
        (copy(c0.at[16], c0.at[0], 6, north), has_n, has_s),
        (copy(c0.at[3], c0.at[19], 7, south), has_s, has_n),
    )
    rows = (
        (copy(fm0.at[pl.ds(16, 2)], fm0.at[pl.ds(0, 2)], 8, north), has_n, has_s),
        (copy(fm0.at[pl.ds(2, 2)], fm0.at[pl.ds(18, 2)], 9, south), has_s, has_n),
    )
    packs = (
        (copy(xo, xw, 10, east), has_e, has_w),
        (copy(xo, xe, 11, west), has_w, has_e),
        (copy(xo.at[15], xc.at[0], 12, targets[4][1]), has_n & has_e, has_s & has_w),
        (copy(xo.at[15], xc.at[1], 13, targets[5][1]), has_n & has_w, has_s & has_e),
        (copy(xo.at[0], xc.at[2], 14, targets[6][1]), has_s & has_e, has_n & has_w),
        (copy(xo.at[0], xc.at[3], 15, targets[7][1]), has_s & has_w, has_n & has_e),
    )

    def start(group_of):
        for one, sends, _ in group_of:
            @pl.when(sends)
            def _(one=one):
                one.start()

    def arrive(group_of):
        for one, _, receives in group_of:
            @pl.when(receives)
            def _(one=one):
                one.wait_recv()

    def sent(group_of):
        for one, sends, _ in group_of:
            @pl.when(sends)
            def _(one=one):
                one.wait_send()

    for one in to_partner:
        one.start()
    start(near)

    for here, ref, at, length in (
        (has_s, c0, 0, 2), (has_n, c0, 18, 2), (has_s, fm0, 0, 2), (has_n, fm0, 18, 2),
        (has_w, xw, 0, 16), (has_e, xe, 0, 16),
        (has_s & has_w, xc, 0, 1), (has_s & has_e, xc, 1, 1),
        (has_n & has_w, xc, 2, 1), (has_n & has_e, xc, 3, 1),
    ):
        @pl.when(jnp.logical_not(here))
        def _(ref=ref, at=at, length=length):
            def clear(r, carry):
                ref[at + r] = jnp.zeros(ref.shape[1:], jnp.float32)
                return carry

            lax.fori_loop(0, length, clear, 0)

    spread = (
        lax.broadcasted_iota(jnp.int32, (128, NT), 0) // 8
        == lax.broadcasted_iota(jnp.int32, (128, NT), 1)
    ).astype(jnp.float32)
    tall = jnp.dot(
        spread, rates[...], precision=lax.Precision.HIGHEST, preferred_element_type=jnp.float32
    )
    square = lax.dot_general(
        tall, spread, (((1,), (1,)), ((), ())), precision=lax.Precision.HIGHEST,
        preferred_element_type=jnp.float32,
    )
    same = lax.rem(lax.broadcasted_iota(jnp.int32, (128, 128), 0), 8) == lax.rem(
        lax.broadcasted_iota(jnp.int32, (128, 128), 1), 8
    )
    wmat[...] = jnp.where(same, square, 0.0)

    def fill(first, field_u, field_v, field_h, field_b, field_s):
        for r in range(8):
            base = field_b[r : r + 1, :].astype(jnp.float32)
            wet = (level_f < jnp.broadcast_to(base, (NZ, 128))).astype(jnp.float32)
            i = first + r
            fm0[i, 0] = field_u[r] * wet
            fm0[i, 1] = field_v[r] * wet
            fm0[i, 2] = field_h[r] * wet
            light = jnp.broadcast_to(field_s[r : r + 1, :], (NZ, 128))
            fm0[i, 3] = jnp.where(level == 0, jnp.broadcast_to(base, (NZ, 128)), light)

    def turn(x):
        return jnp.swapaxes(x, 0, 1)

    fill(
        2 + 8 * half,
        turn(flow[0, :, :, own_half]), turn(flow[1, :, :, own_half]), turn(temp[:, :, own_half]),
        bot[:, own_half], sun[:, own_half],
    )
    for one in to_partner:
        one.wait_recv()
    fill(10 - 8 * half, turn(pf[0]), turn(pf[1]), turn(pt[...]), pb[...], ps[...])
    start(rows)

    def pack(j, carry):
        i = j + 2
        acc = zero
        for n in range(NT):
            x = c0[i, n]
            acc = jnp.where((lane // 2) == (8 * n + 2) // 2, roll(x, 8 * n + 2), acc)
            acc = jnp.where((lane // 2) == (8 * n + 4) // 2, roll(x, 8 * n + 6), acc)
        for f in range(4):
            x = fm0[i, f]
            acc = jnp.where((lane // 2) == (8 * f + 6) // 2, roll(x, 8 * f + 6), acc)
            acc = jnp.where((lane // 2) == (8 * f + 8) // 2, roll(x, 8 * f + 10), acc)
        xo[j] = acc
        return carry

    lax.fori_loop(0, 16, pack, 0)
    start(packs)
    start(far)

    arrive(rows)
    arrive(packs)

    def spread_field(x, f):
        y = jnp.where(lane < 8, roll(x, -8 * f), 0.0)
        for by in (8, 16, 32, 64):
            y = y + roll(y, by)
        return y

    def unpack(i, own, w, e):
        p0[i] = jnp.where(group < 2, roll(w, -4), jnp.where(group >= 6, roll(e, 4), own))
        fields = jnp.where(group < 2, roll(w, -8), jnp.where(group >= 6, e, roll(own, -4)))
        for f in range(4):
            fp0[i, f] = spread_field(fields, f)

    def unpack_row(j, carry):
        unpack(j + 2, xo[j], xw[j], xe[j])
        return carry

    lax.fori_loop(0, 16, unpack_row, 0)
    unpack(1, zero, xc[0], xc[1])
    unpack(18, zero, xc[2], xc[3])
    for i in (0, 19):
        p0[i] = zero
        for f in range(4):
            fp0[i, f] = zero

    def wet_of(aux):
        return (level_f < jnp.broadcast_to(aux[0:1, :], (NZ, 128))).astype(jnp.float32)

    def light_of(aux):
        return jnp.broadcast_to(aux[1:2, :], (NZ, 128))

    def shear_pressure(u, v, h):
        du = u - roll(u, 7, 0)
        dv = v - roll(v, 7, 0)
        q = jnp.where(level < NZ - 1, du * du + dv * dv, 0.0)
        kappa = kappa_base + kappa_shear * q / (1.0 + q)
        total = h
        for by in (1, 2, 4):
            total = total + jnp.where(level >= by, roll(total, by, 0), 0.0)
        return kappa, -expansion * total

    def prepare(fm, fp, first, last):
        def one(i, carry):
            for f, k in ((fm, kpm), (fp, kpp)):
                kappa, pressure = shear_pressure(f[i, 0], f[i, 1], f[i, 2])
                k[i, 0] = kappa
                k[i, 1] = pressure
            return carry

        lax.fori_loop(first, last, one, 0)

    def east_of(m, p, n=0):
        return jnp.where(lane == 127, roll(p, 121 - 8 * n), roll(m, 127))

    def west_of(m, p, n=0):
        return jnp.where(lane == 0, roll(p, 127 - 8 * n), roll(m, 1))

    def apply(a, x, xe_, xw_, xn, xs):
        return (
            a[0] * x + a[1] * xe_ + a[2] * xw_ + a[3] * xn + a[4] * xs
            + a[5] * roll(x, 1, 0) + a[6] * roll(x, 7, 0)
        )

    def flow_row(i, f, k, aux, e_of, w_of, coriolis):
        u, v, h = f[i, 0], f[i, 1], f[i, 2]
        kappa, pressure = k[i, 0], k[i, 1]
        un, us = f[i + 1, 0], f[i - 1, 0]
        vn, vs = f[i + 1, 1], f[i - 1, 1]
        wet = wet_of(aux[i, 3])
        wet_e = w_e = e_of(3)
        wet_w = w_of(3)
        oe = wet * wet_e
        ow = wet * wet_w
        on = wet * wet_of(aux[i + 1, 3])
        os = wet * wet_of(aux[i - 1, 3])
        ue, uw, ve, vw = e_of(0), w_of(0), e_of(1), w_of(1)
        fe = 0.5 * (u + ue) * oe
        fw = 0.5 * (u + uw) * ow
        fn = 0.5 * (v + vn) * on
        fs = 0.5 * (v + vs) * os
        ce = 0.5 * (kappa + e_of(4)) * oe
        cw = 0.5 * (kappa + w_of(4)) * ow
        cn = 0.5 * (kappa + k[i + 1, 0]) * on
        cs = 0.5 * (kappa + k[i - 1, 0]) * os
        lap_u = oe * (ue - u) + ow * (uw - u) + on * (un - u) + os * (us - u)
        lap_v = oe * (ve - v) + ow * (vw - v) + on * (vn - v) + os * (vs - v)
        new_u = wet * (
            u + time_step * (coriolis * v - 0.5 * (e_of(5) - w_of(5)) + viscosity * lap_u)
        )
        new_v = wet * (
            v
            + time_step
            * (-coriolis * u - 0.5 * (k[i + 1, 1] - k[i - 1, 1]) + viscosity * lap_v)
        )
        div = fe - fw + fn - fs
        total = div
        for by in (1, 2, 4):
            total = total + jnp.where(level < NZ - by, roll(total, NZ - by, 0), 0.0)
        w_top = jnp.where(level >= 1, -total, 0.0)
        w_bot = jnp.where(level < NZ - 1, -roll(total, NZ - 1, 0), 0.0)
        a = (
            wet
            * (
                1.0
                - time_step * (ce + cw + cn + cs)
                - 0.5 * time_step * (div + w_top - w_bot)
            ),
            time_step * (ce - 0.5 * fe),
            time_step * (cw + 0.5 * fw),
            time_step * (cn - 0.5 * fn),
            time_step * (cs + 0.5 * fs),
            (-0.5 * time_step) * w_top * wet,
            (0.5 * time_step) * w_bot * wet,
        )
        moved = apply(a, h, e_of(2), w_of(2), f[i + 1, 2], f[i - 1, 2])
        return a, new_u, new_v, moved

    first_lat = 8 * n_row

    def coriolis_of(i):
        latitude = (16 * chip + i - 2).astype(jnp.float32)
        return coriolis_base * (2.0 * (latitude + 0.5) / first_lat - 1.0)

    def main_shift(i, fm, fp, of):
        def one(f):
            if f == 3:
                return of(wet_of(fm0[i, 3]), wet_of(fp0[i, 3]))
            if f >= 4:
                return of(kpm[i, f - 4], kpp[i, f - 4])
            return of(fm[i, f], fp[i, f])

        return one

    def packed_shift(i, fp, by):
        def one(f):
            if f == 3:
                return roll(wet_of(fp0[i, 3]), by)
            if f >= 4:
                return roll(kpp[i, f - 4], by)
            return roll(fp[i, f], by)

        return one

    def flow_main(i, fm, fp, fm_new):
        a, u, v, h = flow_row(
            i, fm, kpm, fm0, main_shift(i, fm, fp, east_of), main_shift(i, fm, fp, west_of),
            coriolis_of(i),
        )
        for s in range(7):
            am[i, s] = a[s]
        fm_new[i, 0] = u
        fm_new[i, 1] = v
        fm_new[i, 2] = h

    def flow_packed(i, fp, fp_new):
        a, u, v, h = flow_row(
            i, fp, kpp, fp0, packed_shift(i, fp, 127), packed_shift(i, fp, 1), coriolis_of(i)
        )
        for s in range(7):
            ap[i, s] = a[s]
        fp_new[i, 0] = u
        fp_new[i, 1] = v
        fp_new[i, 2] = h

    def profile_of(pigment):
        squared = pigment * pigment
        depth = water_absorb + pigment_absorb * squared / (1.0 + squared)
        above = zero
        for by in (1, 2, 3):
            above = above + jnp.where(level >= by, roll(depth, by, 0), 0.0)
        return jnp.where(
            level < KL, jnp.exp(-above) * (1.0 - jnp.exp(-depth)), 0.0
        )

    def tracer_row(i, c, p, c_new, i_new, fm_new):
        a = [am[i, s] for s in range(7)]
        wet = wet_of(fm0[i, 3])
        ghost = p[i]
        moved = []
        for n in range(NT):
            x = c[i, n]
            moved.append(
                apply(a, x, east_of(x, ghost, n), west_of(x, ghost, n), c[i + 1, n], c[i - 1, n])
            )
        bent = jnp.concatenate([m * lax.rsqrt(1.0 + m * m) for m in moved], axis=0)
        coupling = jnp.dot(
            wmat[...], bent, precision=lax.Precision.HIGHEST, preferred_element_type=jnp.float32
        )
        scale = react_step * wet
        for n in range(NT):
            value = moved[n] + scale * coupling[8 * n : 8 * n + 8]
            c_new[i_new, n] = value
            if n == 0:
                fm_new[i, 2] = fm_new[i, 2] + heat_gain * light_of(fm0[i, 3]) * wet * profile_of(
                    value
                )

    prepare(fm0, fp0, 0, 20)

    def step1_flow(i, carry):
        flow_main(i, fm0, fp0, fm1)
        flow_packed(i, fp0, fp1)
        return carry

    lax.fori_loop(1, 19, step1_flow, 0)

    def step1_packed(i, carry):
        x = p0[i]
        a = [ap[i, s] for s in range(7)]
        m = apply(a, x, roll(x, 127), roll(x, 1), p0[i + 1], p0[i - 1])
        p1[i] = m
        psat[pl.ds(pl.multiple_of(8 * (i - 2), 8), 8), :] = m * lax.rsqrt(1.0 + m * m)
        return carry

    lax.fori_loop(2, 18, step1_packed, 0)
    psat[...] = lax.dot_general(
        psat[...], wmat[...], (((1,), (1,)), ((), ())), precision=lax.Precision.HIGHEST,
        preferred_element_type=jnp.float32,
    )

    def step1_react(i, carry):
        wet = wet_of(fp0[i, 3])
        value = p1[i] + react_step * wet * psat[pl.ds(pl.multiple_of(8 * (i - 2), 8), 8), :]
        p1[i] = value
        fp1[i, 2] = fp1[i, 2] + heat_gain * light_of(fp0[i, 3]) * wet * profile_of(
            spread_field(value, 0)
        )
        return carry

    lax.fori_loop(2, 18, step1_react, 0)

    arrive(near)

    def step1_main(i, carry):
        tracer_row(i, c0, p0, c1, i, fm1)
        return carry

    lax.fori_loop(2, 18, step1_main, 0)

    prepare(fm1, fp1, 2, 18)

    def step2_main(i, carry):
        flow_main(i, fm1, fp1, fm0_next)
        tracer_row(i, c1, p1, c2, i - 2, fm0_next)
        return carry

    fm0_next = ap_flow
    lax.fori_loop(3, 17, step2_main, 0)

    arrive(far)
    step1_main(1, 0)
    step1_main(18, 0)

    def prepare_main(i):
        kappa, pressure = shear_pressure(fm1[i, 0], fm1[i, 1], fm1[i, 2])
        kpm[i, 0] = kappa
        kpm[i, 1] = pressure

    prepare_main(1)
    prepare_main(18)
    step2_main(2, 0)
    step2_main(17, 0)

    mine = 2 + 8 * half
    theirs = 10 - 8 * half
    for f in range(3):
        fo[f] = turn(fm0_next[pl.ds(theirs, 8), f])
    back = copy(fo, fr, 16, partner)
    back.start()

    def turn_out(n, carry):
        for t in range(2):
            tr_out[0, n, :, 8 * t : 8 * t + 8, :] = jnp.swapaxes(c2[8 * t : 8 * t + 8, n], 0, 1)
        return carry

    lax.fori_loop(0, NT, turn_out, 0)
    for f in range(2):
        flow_out[f, :, :, own_half] = turn(fm0_next[pl.ds(mine, 8), f])
    temp_out[:, :, own_half] = turn(fm0_next[pl.ds(mine, 8), 2])
    back.wait_recv()
    for f in range(2):
        flow_out[f, :, :, other_half] = fr[f]
    temp_out[:, :, other_half] = fr[2]
    for one in to_partner:
        one.wait_send()
    sent(near)
    sent(rows)
    sent(packs)
    sent(far)
    back.wait_send()


def on_device(n_row, n_col, *args):
    f32 = jnp.float32
    vmem = pl.BlockSpec(memory_space=pltpu.VMEM)
    tile = (NZ, 128)
    return tuple(
        pl.pallas_call(
            functools.partial(kernel, n_row, n_col),
            out_shape=(
                jax.ShapeDtypeStruct((2, NZ, 8, 256), f32),
                jax.ShapeDtypeStruct((NZ, 8, 256), f32),
                jax.ShapeDtypeStruct((1, NT, NZ, 16, 128), f32),
            ),
            in_specs=[vmem] * 6,
            out_specs=(vmem, vmem, vmem),
            scratch_shapes=[
                pltpu.VMEM((20, NT) + tile, f32),
                pltpu.VMEM((20, NT) + tile, f32),
                pltpu.VMEM((16, NT) + tile, f32),
                pltpu.VMEM((20,) + tile, f32),
                pltpu.VMEM((20,) + tile, f32),
                pltpu.VMEM((128, 128), f32),
                pltpu.VMEM((20, 4) + tile, f32),
                pltpu.VMEM((20, 4) + tile, f32),
                pltpu.VMEM((20, 3) + tile, f32),
                pltpu.VMEM((20, 3) + tile, f32),
                pltpu.VMEM((20, 2) + tile, f32),
                pltpu.VMEM((20, 2) + tile, f32),
                pltpu.VMEM((20, 7) + tile, f32),
                pltpu.VMEM((20, 7) + tile, f32),
                pltpu.VMEM((20, 3) + tile, f32),
                pltpu.VMEM((128, 128), f32),
                pltpu.VMEM((16,) + tile, f32),
                pltpu.VMEM((16,) + tile, f32),
                pltpu.VMEM((16,) + tile, f32),
                pltpu.VMEM((4,) + tile, f32),
                pltpu.VMEM((2, NZ, 8, 128), f32),
                pltpu.VMEM((NZ, 8, 128), f32),
                pltpu.VMEM((8, 128), jnp.int32),
                pltpu.VMEM((8, 128), f32),
                pltpu.VMEM((3, NZ, 8, 128), f32),
                pltpu.VMEM((3, NZ, 8, 128), f32),
                pltpu.SemaphoreType.DMA((17,)),
                pltpu.SemaphoreType.DMA((17,)),
            ],
            compiler_params=pltpu.CompilerParams(collective_id=0, has_side_effects=True),
        )(*args)
    )


def solution(mesh):
    in_specs = (
        P(None, None, "row", "col"),
        P(None, "row", "col"),
        P("row", None, None, None, "col"),
        P("row", "col"),
        P("row", "col"),
        P(),
    )
    out_specs = (
        P(None, None, "row", "col"),
        P(None, "row", "col"),
        P("row", None, None, None, "col"),
    )
    return jax.shard_map(
        functools.partial(on_device, mesh.shape["row"], mesh.shape["col"]),
        mesh=mesh, in_specs=in_specs, out_specs=out_specs, check_vma=False,
    )
```

time: 165 us -> 71.7 us (0.43)
  the two profiles are of different devices: /device:TPU:33 before, /device:TPU:7 now
where the time goes in v1:
time: 71.7 us; the launch traced here: 71.5 us
  Pallas kernels  66.3 us (92%)
  local copies, waits for them, and re-layouts  4.53 us (6%)
    pallas_call x1, Pallas kernels, on_device(): pl.pallas_call(functools.partial(kernel, n_row, n_col), out_shape=(jax.Sh...  66.3 us
    unnamed x5, local copies, waits for them, and re-layouts  4.53 us

profile of v1, /device:TPU:7, one launch (start us, length us, event | category | flops | bytes accessed | tf_op | source)
XLA Modules:
  0.0 71.5 jit_solution(3663705026990078433)
XLA Ops:
  0.6 66.3 %shard_map.85 = (f32[2,8,8,256]{3,2,1,0:T(8,128)}, f32[8,8,256]{2,1,0:T(8,128)}, f32[1,16,8,16,128]{4,3,2,1,0:T(8,128)}) custom-call(f32[2,8,8,256]{3,2,1,0:T(8,128)} %flow.1, f32[8,8,256]{2,1,0:T(8,128)} %temp.1, f32[1,16,8,16,128]{4,3,2,1,0:T(8,128)} %tr.1, s32[8,256]{1,0:T(8,128)} %bot.1, f32[8,256]{1,0:T(8,128)} %sun.1, f32[16,16]{1,0:T(8,128)} %rates.1), custom_call_target="tpu_custom_call" | custom-call | tf_op jit(solution)/shard_map/pallas_call | solution.py:513
  66.9 0.0 copy-start
  66.9 1.6 %copy.12 = f32[2,8,8,256]{3,2,1,0:T(8,128)} copy(f32[2,8,8,256]{3,2,1,0:T(8,128)} %get-tuple-element.6) | data formatting | bytes 262144
  68.5 0.0 copy-done
  68.5 0.6 copy.13
  69.2 2.3 %copy.14 = f32[1,16,8,16,128]{4,3,2,1,0:T(8,128)} copy(f32[1,16,8,16,128]{4,3,2,1,0:T(8,128)} %get-tuple-element.8) | data formatting | bytes 2097152
Async XLA Ops:
  66.9 1.6 %copy-start = (f32[8,8,256]{2,1,0:T(8,128)S(1)}, f32[8,8,256]{2,1,0:T(8,128)}, u32[]{:S(2)}) copy-start(f32[8,8,256]{2,1,0:T(8,128)} %get-tuple-element.7) | copy-start | bytes 196612

commit v2 on v1

v2 whole, which is shorter than its diff:
```python
import functools

import jax
import jax.numpy as jnp
from jax import lax
from jax.experimental import pallas as pl
from jax.experimental.pallas import tpu as pltpu
from jax.sharding import PartitionSpec as P

MESH = pl.DeviceIdType.MESH
NT = 16
NZ = 8
KL = 4
PERIOD = 4

time_step = 0.2
viscosity = 0.2
expansion = 0.05
coriolis_base = 0.5
kappa_base = 0.05
kappa_shear = 0.2
react_step = 0.25
water_absorb = 0.1
pigment_absorb = 0.6
heat_gain = 1.0


def kernel(
    n_row, n_col,
    flow, temp, tr, bot, sun, rates,
    c2, mine_out, theirs_out,
    c0, c1, p0, p1, psat, fm0, fp0, fm1, fp1, fm2, kpm, kpp, kpm1, kpp1, am, ap, wmat,
    xo, xw, xe, px_out, px_in, pf, pt, pb, ps, fr,
    send, recv, ready,
):
    row = lax.axis_index("row")
    col = lax.axis_index("col")
    half = lax.rem(row, 2)
    chip = row // 2
    other = 2 * chip + 1 - half
    west_col = col - 1 + half
    east_col = col + half
    has_w = west_col >= 0
    has_e = east_col < n_col
    has_n = row + 2 < n_row
    has_s = row >= 2
    partner = (other, col)
    west = (other, west_col)
    east = (other, east_col)
    north = (row + 2, col)
    south = (row - 2, col)
    place = lax.rem(chip, PERIOD)
    late_n = has_n & (place != PERIOD - 1)
    late_s = has_s & (place == 0)
    soon_n = has_n & (place == PERIOD - 1)
    soon_s = has_s & (place != 0)

    barrier = pltpu.get_barrier_semaphore()
    for tells, target in ((has_e, east), (has_w, west), (late_n, north), (late_s, south)):
        @pl.when(tells)
        def _(target=target):
            pl.semaphore_signal(barrier, inc=1, device_id=target, device_id_type=MESH)

    count = jnp.int32(0)
    for waits in (has_e, has_w, soon_n, soon_s):
        count = count + waits.astype(jnp.int32)

    lane = lax.broadcasted_iota(jnp.int32, (NZ, 128), 1)
    level = lax.broadcasted_iota(jnp.int32, (NZ, 128), 0)
    level_f = level.astype(jnp.float32)
    group = lax.rem(lane, 8)
    zero = jnp.zeros((NZ, 128), jnp.float32)

    def roll(x, by, axis=1):
        by = by % x.shape[axis]
        return pltpu.roll(x, by, axis) if by else x

    def turn_in(n, carry):
        for t in range(2):
            c0[pl.ds(2 + 8 * t, 8), n] = jnp.swapaxes(tr[0, n, :, 8 * t : 8 * t + 8, :], 0, 1)
        return carry

    lax.fori_loop(0, NT, turn_in, 0)

    def copy(src, dst, k, target):
        return pltpu.make_async_remote_copy(
            src_ref=src, dst_ref=dst, send_sem=send.at[k], recv_sem=recv.at[k],
            device_id=target, device_id_type=MESH,
        )

    own_half = pl.ds(pl.multiple_of(half * 128, 128), 128)
    other_half = pl.ds(pl.multiple_of((1 - half) * 128, 128), 128)
    to_partner = (
        copy(flow.at[:, :, :, other_half], pf, 0, partner),
        copy(temp.at[:, :, other_half], pt, 1, partner),
        copy(bot.at[:, other_half], pb, 2, partner),
        copy(sun.at[:, other_half], ps, 3, partner),
    )
    to_east = copy(xo, xw, 4, east)
    to_west = copy(xo, xe, 5, west)
    near_n = copy(c0.at[17], c0.at[1], 6, north)
    near_s = copy(c0.at[2], c0.at[18], 7, south)
    far_n = copy(c0.at[16], c0.at[0], 8, north)
    far_s = copy(c0.at[3], c0.at[19], 9, south)
    rows_n = copy(fm0.at[pl.ds(16, 2)], fm0.at[pl.ds(0, 2)], 10, north)
    rows_s = copy(fm0.at[pl.ds(2, 2)], fm0.at[pl.ds(18, 2)], 11, south)
    edge_n = copy(px_out.at[1], px_in.at[0], 12, north)
    edge_s = copy(px_out.at[0], px_in.at[1], 13, south)

    def start(here, *copies):
        @pl.when(here)
        def _():
            for one in copies:
                one.start()

    for here, ref, at, length in (
        (has_s, c0, 0, 2), (has_n, c0, 18, 2), (has_s, fm0, 0, 2), (has_n, fm0, 18, 2),
        (has_w, xw, 0, 16), (has_e, xe, 0, 16), (has_s, px_in, 0, 1), (has_n, px_in, 1, 1),
    ):
        @pl.when(jnp.logical_not(here))
        def _(ref=ref, at=at, length=length):
            def clear(r, carry):
                ref[at + r] = jnp.zeros(ref.shape[1:], jnp.float32)
                return carry

            lax.fori_loop(0, length, clear, 0)

    pl.semaphore_wait(barrier, count)
    for one in to_partner:
        one.start()
    for here, target, k in ((soon_s, south, 0), (soon_n, north, 1)):
        @pl.when(here)
        def _(target=target, k=k):
            pl.semaphore_signal(ready.at[k], inc=1, device_id=target, device_id_type=MESH)

    start(soon_n, near_n, far_n)
    start(soon_s, near_s, far_s)

    spread = (
        lax.broadcasted_iota(jnp.int32, (128, NT), 0) // 8
        == lax.broadcasted_iota(jnp.int32, (128, NT), 1)
    ).astype(jnp.float32)
    tall = jnp.dot(
        spread, rates[...], precision=lax.Precision.HIGHEST, preferred_element_type=jnp.float32
    )
    square = lax.dot_general(
        tall, spread, (((1,), (1,)), ((), ())), precision=lax.Precision.HIGHEST,
        preferred_element_type=jnp.float32,
    )
    same = lax.rem(lax.broadcasted_iota(jnp.int32, (128, 128), 0), 8) == lax.rem(
        lax.broadcasted_iota(jnp.int32, (128, 128), 1), 8
    )
    wmat[...] = jnp.where(same, square, 0.0)

    def fill(first, field_u, field_v, field_h, field_b, field_s):
        for r in range(8):
            base = field_b[r : r + 1, :].astype(jnp.float32)
            wet = (level_f < jnp.broadcast_to(base, (NZ, 128))).astype(jnp.float32)
            i = first + r
            fm0[i, 0] = field_u[r] * wet
            fm0[i, 1] = field_v[r] * wet
            fm0[i, 2] = field_h[r] * wet
            light = jnp.broadcast_to(field_s[r : r + 1, :], (NZ, 128))
            fm0[i, 3] = jnp.where(level == 0, jnp.broadcast_to(base, (NZ, 128)), light)

    def turn(x):
        return jnp.swapaxes(x, 0, 1)

    fill(
        2 + 8 * half,
        turn(flow[0, :, :, own_half]), turn(flow[1, :, :, own_half]), turn(temp[:, :, own_half]),
        bot[:, own_half], sun[:, own_half],
    )
    for one in to_partner:
        one.wait_recv()
    fill(10 - 8 * half, turn(pf[0]), turn(pf[1]), turn(pt[...]), pb[...], ps[...])
    start(soon_n, rows_n)
    start(soon_s, rows_s)

    def pack(j, carry):
        i = j + 2
        acc = zero
        for n in range(NT):
            x = c0[i, n]
            acc = jnp.where((lane // 2) == (8 * n + 2) // 2, roll(x, 8 * n + 2), acc)
            acc = jnp.where((lane // 2) == (8 * n + 4) // 2, roll(x, 8 * n + 6), acc)
        for f in range(4):
            x = fm0[i, f]
            acc = jnp.where((lane // 2) == (8 * f + 6) // 2, roll(x, 8 * f + 6), acc)
            acc = jnp.where((lane // 2) == (8 * f + 8) // 2, roll(x, 8 * f + 10), acc)
        xo[j] = acc
        return carry

    lax.fori_loop(0, 16, pack, 0)
    start(has_e, to_east)
    start(has_w, to_west)

    @pl.when(has_w)
    def _():
        to_east.wait_recv()

    @pl.when(has_e)
    def _():
        to_west.wait_recv()

    def spread_field(x, f):
        y = jnp.where(lane < 8, roll(x, -8 * f), 0.0)
        for by in (8, 16, 32, 64):
            y = y + roll(y, by)
        return y

    def unpack_row(j, carry):
        own, w, e = xo[j], xw[j], xe[j]
        p0[j + 2] = jnp.where(group < 2, roll(w, -4), jnp.where(group >= 6, roll(e, 4), own))
        fields = fields_of(j)
        for f in range(4):
            fp0[j + 2, f] = spread_field(fields, f)
        return carry

    def fields_of(j):
        return jnp.where(group < 2, roll(xw[j], -8), jnp.where(group >= 6, xe[j], roll(xo[j], -4)))

    lax.fori_loop(0, 16, unpack_row, 0)
    for side, j in ((0, 0), (1, 15)):
        px_out[side, 0] = p0[j + 2]
        px_out[side, 1] = fields_of(j)
    start(soon_n, edge_n)
    start(soon_s, edge_s)

    @pl.when(late_n)
    def _():
        pl.semaphore_wait(ready.at[0], 1)
        for one in (near_n, rows_n, far_n, edge_n):
            one.start()

    def wet_of(aux):
        return (level_f < jnp.broadcast_to(aux[0:1, :], (NZ, 128))).astype(jnp.float32)

    def light_of(aux):
        return jnp.broadcast_to(aux[1:2, :], (NZ, 128))

    def shear_pressure(u, v, h):
        du = u - roll(u, 7, 0)
        dv = v - roll(v, 7, 0)
        q = jnp.where(level < NZ - 1, du * du + dv * dv, 0.0)
        kappa = kappa_base + kappa_shear * q / (1.0 + q)
        total = h
        for by in (1, 2, 4):
            total = total + jnp.where(level >= by, roll(total, by, 0), 0.0)
        return kappa, -expansion * total

    def prepare_row(i, f, k):
        kappa, pressure = shear_pressure(f[i, 0], f[i, 1], f[i, 2])
        k[i, 0] = kappa
        k[i, 1] = pressure

    def prepare(fm, fp, km, kp, first, last):
        def one(i, carry):
            prepare_row(i, fm, km)
            prepare_row(i, fp, kp)
            return carry

        lax.fori_loop(first, last, one, 0)

    def east_of(m, p, n=0):
        return jnp.where(lane == 127, roll(p, 121 - 8 * n), roll(m, 127))

    def west_of(m, p, n=0):
        return jnp.where(lane == 0, roll(p, 127 - 8 * n), roll(m, 1))

    def apply(a, x, xe_, xw_, xn, xs):
        return (
            a[0] * x + a[1] * xe_ + a[2] * xw_ + a[3] * xn + a[4] * xs
            + a[5] * roll(x, 1, 0) + a[6] * roll(x, 7, 0)
        )

    def flow_row(i, f, k, aux, e_of, w_of, coriolis):
        u, v, h = f[i, 0], f[i, 1], f[i, 2]
        kappa, pressure = k[i, 0], k[i, 1]
        un, us = f[i + 1, 0], f[i - 1, 0]
        vn, vs = f[i + 1, 1], f[i - 1, 1]
        wet = wet_of(aux[i, 3])
        wet_e = w_e = e_of(3)
        wet_w = w_of(3)
        oe = wet * wet_e
        ow = wet * wet_w
        on = wet * wet_of(aux[i + 1, 3])
        os = wet * wet_of(aux[i - 1, 3])
        ue, uw, ve, vw = e_of(0), w_of(0), e_of(1), w_of(1)
        fe = 0.5 * (u + ue) * oe
        fw = 0.5 * (u + uw) * ow
        fn = 0.5 * (v + vn) * on
        fs = 0.5 * (v + vs) * os
        ce = 0.5 * (kappa + e_of(4)) * oe
        cw = 0.5 * (kappa + w_of(4)) * ow
        cn = 0.5 * (kappa + k[i + 1, 0]) * on
        cs = 0.5 * (kappa + k[i - 1, 0]) * os
        lap_u = oe * (ue - u) + ow * (uw - u) + on * (un - u) + os * (us - u)
        lap_v = oe * (ve - v) + ow * (vw - v) + on * (vn - v) + os * (vs - v)
        new_u = wet * (
            u + time_step * (coriolis * v - 0.5 * (e_of(5) - w_of(5)) + viscosity * lap_u)
        )
        new_v = wet * (
            v
            + time_step
            * (-coriolis * u - 0.5 * (k[i + 1, 1] - k[i - 1, 1]) + viscosity * lap_v)
        )
        div = fe - fw + fn - fs
        total = div
        for by in (1, 2, 4):
            total = total + jnp.where(level < NZ - by, roll(total, NZ - by, 0), 0.0)
        w_top = jnp.where(level >= 1, -total, 0.0)
        w_bot = jnp.where(level < NZ - 1, -roll(total, NZ - 1, 0), 0.0)
        a = (
            wet
            * (
                1.0
                - time_step * (ce + cw + cn + cs)
                - 0.5 * time_step * (div + w_top - w_bot)
            ),
            time_step * (ce - 0.5 * fe),
            time_step * (cw + 0.5 * fw),
            time_step * (cn - 0.5 * fn),
            time_step * (cs + 0.5 * fs),
            (-0.5 * time_step) * w_top * wet,
            (0.5 * time_step) * w_bot * wet,
        )
        moved = apply(a, h, e_of(2), w_of(2), f[i + 1, 2], f[i - 1, 2])
        return a, new_u, new_v, moved

    first_lat = 8 * n_row

    def coriolis_of(i):
        latitude = (16 * chip + i - 2).astype(jnp.float32)
        return coriolis_base * (2.0 * (latitude + 0.5) / first_lat - 1.0)

    def main_shift(i, fm, fp, km, kp, of):
        def one(f):
            if f == 3:
                return of(wet_of(fm0[i, 3]), wet_of(fp0[i, 3]))
            if f >= 4:
                return of(km[i, f - 4], kp[i, f - 4])
            return of(fm[i, f], fp[i, f])

        return one

    def packed_shift(i, by):
        def one(f):
            if f == 3:
                return roll(wet_of(fp0[i, 3]), by)
            if f >= 4:
                return roll(kpp[i, f - 4], by)
            return roll(fp0[i, f], by)

        return one

    def keep(i, result, a_new, f_new):
        a, u, v, h = result
        for s in range(7):
            a_new[i, s] = a[s]
        f_new[i, 0] = u
        f_new[i, 1] = v
        f_new[i, 2] = h

    def flow_main(i, fm, fp, km, kp, f_new):
        keep(
            i,
            flow_row(
                i, fm, km, fm0, main_shift(i, fm, fp, km, kp, east_of),
                main_shift(i, fm, fp, km, kp, west_of), coriolis_of(i),
            ),
            am, f_new,
        )

    def flow_packed(i):
        keep(
            i,
            flow_row(i, fp0, kpp, fp0, packed_shift(i, 127), packed_shift(i, 1), coriolis_of(i)),
            ap, fp1,
        )

    def profile_of(pigment):
        squared = pigment * pigment
        depth = water_absorb + pigment_absorb * squared / (1.0 + squared)
        above = zero
        for by in (1, 2, 3):
            above = above + jnp.where(level >= by, roll(depth, by, 0), 0.0)
        return jnp.where(
            level < KL, jnp.exp(-above) * (1.0 - jnp.exp(-depth)), 0.0
        )

    def tracer_row(i, c, p, c_new, i_new, fm_new):
        a = [am[i, s] for s in range(7)]
        wet = wet_of(fm0[i, 3])
        ghost = p[i]
        moved = []
        for n in range(NT):
            x = c[i, n]
            moved.append(
                apply(a, x, east_of(x, ghost, n), west_of(x, ghost, n), c[i + 1, n], c[i - 1, n])
            )
        bent = jnp.concatenate([m * lax.rsqrt(1.0 + m * m) for m in moved], axis=0)
        coupling = jnp.dot(
            wmat[...], bent, precision=lax.Precision.HIGHEST, preferred_element_type=jnp.float32
        )
        scale = react_step * wet
        for n in range(NT):
            value = moved[n] + scale * coupling[8 * n : 8 * n + 8]
            c_new[i_new, n] = value
            if n == 0:
                fm_new[i, 2] = fm_new[i, 2] + heat_gain * light_of(fm0[i, 3]) * wet * profile_of(
                    value
                )

    def step1_flow(i, carry):
        flow_main(i, fm0, fp0, kpm, kpp, fm1)
        flow_packed(i)
        return carry

    def packed_moved(i):
        x = p0[i]
        a = [ap[i, s] for s in range(7)]
        m = apply(a, x, roll(x, 127), roll(x, 1), p0[i + 1], p0[i - 1])
        p1[i] = m
        return m * lax.rsqrt(1.0 + m * m)

    def couple(x):
        return lax.dot_general(
            x, wmat[...], (((1,), (1,)), ((), ())), precision=lax.Precision.HIGHEST,
            preferred_element_type=jnp.float32,
        )

    def packed_react(i, coupling):
        wet = wet_of(fp0[i, 3])
        value = p1[i] + react_step * wet * coupling
        p1[i] = value
        fp1[i, 2] = fp1[i, 2] + heat_gain * light_of(fp0[i, 3]) * wet * profile_of(
            spread_field(value, 0)
        )

    def step1_main(i, carry):
        tracer_row(i, c0, p0, c1, i, fm1)
        return carry

    def step2_main(i, carry):
        flow_main(i, fm1, fp1, kpm1, kpp1, fm2)
        tracer_row(i, c1, p1, c2, i - 2, fm2)
        return carry

    prepare(fm0, fp0, kpm, kpp, 2, 18)
    lax.fori_loop(3, 17, step1_flow, 0)

    def packed_in(i, carry):
        psat[pl.ds(pl.multiple_of(8 * (i - 3), 8), 8), :] = packed_moved(i)
        return carry

    def packed_end(i, carry):
        packed_react(i, psat[pl.ds(pl.multiple_of(8 * (i - 3), 8), 8), :])
        return carry

    lax.fori_loop(3, 17, packed_in, 0)
    psat[...] = couple(psat[...])
    lax.fori_loop(3, 17, packed_end, 0)
    lax.fori_loop(3, 17, step1_main, 0)

    @pl.when(late_s)
    def _():
        pl.semaphore_wait(ready.at[1], 1)
        for one in (near_s, rows_s, far_s, edge_s):
            one.start()

    prepare(fm1, fp1, kpm1, kpp1, 3, 17)
    lax.fori_loop(4, 16, step2_main, 0)

    def finish(out, by, side):
        edge = out + by
        p0[out] = px_in[side, 0]
        for f in range(4):
            fp0[out, f] = spread_field(px_in[side, 1], f)
        prepare_row(out - by, fm0, kpm)
        prepare_row(out, fm0, kpm)
        prepare_row(out, fp0, kpp)
        flow_main(edge, fm0, fp0, kpm, kpp, fm1)
        flow_packed(edge)
        flow_main(out, fm0, fp0, kpm, kpp, fm1)
        packed_react(edge, couple(packed_moved(edge)))
        step1_main(edge, 0)
        step1_main(out, 0)
        prepare_row(edge, fm1, kpm1)
        prepare_row(edge, fp1, kpp1)
        prepare_row(out, fm1, kpm1)
        step2_main(edge + by, 0)
        step2_main(edge, 0)

    @pl.when(has_n)
    def _():
        for one in (near_s, far_s, rows_s, edge_s):
            one.wait_recv()

    finish(18, -1, 1)

    @pl.when(has_s)
    def _():
        for one in (near_n, far_n, rows_n, edge_n):
            one.wait_recv()

    finish(1, 1, 0)

    back = copy(fm2.at[pl.ds(10 - 8 * half, 8)], fr, 14, partner)
    back.start()
    for f in range(3):
        mine_out[:, f] = fm2[pl.ds(2 + 8 * half, 8), f]
    for one in to_partner:
        one.wait_send()
    for here, copies in (
        (has_e, (to_east,)), (has_w, (to_west,)),
        (has_n, (near_n, far_n, rows_n, edge_n)), (has_s, (near_s, far_s, rows_s, edge_s)),
    ):
        @pl.when(here)
        def _(copies=copies):
            for one in copies:
                one.wait_send()

    back.wait()
    theirs_out[...] = fr[...]


def lay_out(c2, mine, theirs, flow_out, temp_out, tr_out):
    half = lax.rem(lax.axis_index("row"), 2)

    def turn_out(n, carry):
        for t in range(2):
            tr_out[0, n, :, 8 * t : 8 * t + 8, :] = jnp.swapaxes(c2[8 * t : 8 * t + 8, n], 0, 1)
        return carry

    lax.fori_loop(0, c2.shape[1], turn_out, 0)

    @pl.when(pl.program_id(0) == 0)
    def _():
        for ref, at in ((mine, half), (theirs, 1 - half)):
            lanes = pl.ds(pl.multiple_of(at * 128, 128), 128)
            for f in range(2):
                flow_out[f, :, :, lanes] = jnp.swapaxes(ref[:, f], 0, 1)
            temp_out[:, :, lanes] = jnp.swapaxes(ref[:, 2], 0, 1)


def on_device(n_row, n_col, *args):
    f32 = jnp.float32
    vmem = pl.BlockSpec(memory_space=pltpu.VMEM)
    tile = (NZ, 128)
    c2, mine, theirs = pl.pallas_call(
        functools.partial(kernel, n_row, n_col),
        out_shape=(
            jax.ShapeDtypeStruct((16, NT) + tile, f32),
            jax.ShapeDtypeStruct((8, 3) + tile, f32),
            jax.ShapeDtypeStruct((8, 3) + tile, f32),
        ),
        in_specs=[vmem] * 6,
        out_specs=(vmem, vmem, vmem),
        scratch_shapes=[
            pltpu.VMEM((20, NT) + tile, f32),
            pltpu.VMEM((20, NT) + tile, f32),
            pltpu.VMEM((20,) + tile, f32),
            pltpu.VMEM((20,) + tile, f32),
            pltpu.VMEM((112, 128), f32),
            pltpu.VMEM((20, 4) + tile, f32),
            pltpu.VMEM((20, 4) + tile, f32),
            pltpu.VMEM((20, 3) + tile, f32),
            pltpu.VMEM((20, 3) + tile, f32),
            pltpu.VMEM((20, 3) + tile, f32),
            pltpu.VMEM((20, 2) + tile, f32),
            pltpu.VMEM((20, 2) + tile, f32),
            pltpu.VMEM((20, 2) + tile, f32),
            pltpu.VMEM((20, 2) + tile, f32),
            pltpu.VMEM((20, 7) + tile, f32),
            pltpu.VMEM((20, 7) + tile, f32),
            pltpu.VMEM((128, 128), f32),
            pltpu.VMEM((16,) + tile, f32),
            pltpu.VMEM((16,) + tile, f32),
            pltpu.VMEM((16,) + tile, f32),
            pltpu.VMEM((2, 2) + tile, f32),
            pltpu.VMEM((2, 2) + tile, f32),
            pltpu.VMEM((2, NZ, 8, 128), f32),
            pltpu.VMEM((NZ, 8, 128), f32),
            pltpu.VMEM((8, 128), jnp.int32),
            pltpu.VMEM((8, 128), f32),
            pltpu.VMEM((8, 3) + tile, f32),
            pltpu.SemaphoreType.DMA((15,)),
            pltpu.SemaphoreType.DMA((15,)),
            pltpu.SemaphoreType.REGULAR((2,)),
        ],
        compiler_params=pltpu.CompilerParams(collective_id=0, has_side_effects=True),
    )(*args)
    small = pl.BlockSpec((8, 3) + tile, lambda g: (0, 0, 0, 0))
    parts = 2
    return tuple(
        pl.pallas_call(
            lay_out,
            grid=(parts,),
            out_shape=(
                jax.ShapeDtypeStruct((2, NZ, 8, 256), f32),
                jax.ShapeDtypeStruct((NZ, 8, 256), f32),
                jax.ShapeDtypeStruct((1, NT, NZ, 16, 128), f32),
            ),
            in_specs=[pl.BlockSpec((16, NT // parts) + tile, lambda g: (0, g, 0, 0)), small, small],
            out_specs=(
                pl.BlockSpec((2, NZ, 8, 256), lambda g: (0, 0, 0, 0)),
                pl.BlockSpec((NZ, 8, 256), lambda g: (0, 0, 0)),
                pl.BlockSpec((1, NT // parts, NZ, 16, 128), lambda g: (0, g, 0, 0, 0)),
            ),
        )(c2, mine, theirs)
    )


def solution(mesh):
    in_specs = (
        P(None, None, "row", "col"),
        P(None, "row", "col"),
        P("row", None, None, None, "col"),
        P("row", "col"),
        P("row", "col"),
        P(),
    )
    out_specs = (
        P(None, None, "row", "col"),
        P(None, "row", "col"),
        P("row", None, None, None, "col"),
    )
    return jax.shard_map(
        functools.partial(on_device, mesh.shape["row"], mesh.shape["col"]),
        mesh=mesh, in_specs=in_specs, out_specs=out_specs, check_vma=False,
    )
```

time: 71.7 us -> 57 us (0.79)
  the two profiles are of different devices: /device:TPU:7 before, /device:TPU:321 now
where the time goes in v2:
time: 57 us; the launch traced here: 56.8 us
  Pallas kernels  56.2 us (99%)
  between operations  0.64 us (1%)
    pallas_call x1, Pallas kernels, on_device(): pl.pallas_call(functools.partial(kernel, n_row, n_col), out_shape=(jax.Sh...  53.9 us
    pallas_call x1, Pallas kernels, on_device(): pl.pallas_call(lay_out, grid=(parts,), out_shape=(jax.ShapeDtypeStruct((2...  2.33 us

profile of v2, /device:TPU:321, one launch (start us, length us, event | category | flops | bytes accessed | tf_op | source)
XLA Modules:
  0.0 56.8 jit_solution(3062889909194619250)
XLA Ops:
  0.6 53.9 %shard_map.85 = (f32[16,16,8,128]{3,2,1,0:T(8,128)}, f32[8,3,8,128]{3,2,1,0:T(8,128)}, f32[8,3,8,128]{3,2,1,0:T(8,128)}) custom-call(f32[2,8,8,256]{3,2,1,0:T(8,128)} %flow.1, f32[8,8,256]{2,1,0:T(8,128)} %temp.1, f32[1,16,8,16,128]{4,3,2,1,0:T(8,128)} %tr.1, s32[8,256]{1,0:T(8,128)} %bot.1, f32[8,256]{1,0:T(8,128)} %sun.1, f32[16,16]{1,0:T(8,128)} %rates.1), custom_call_target="tpu_custom_call" | custom-call | tf_op jit(solution)/shard_map/pallas_call | solution.py:551
  54.5 2.3 %shard_map.86 = (f32[2,8,8,256]{3,2,1,0:T(8,128)}, f32[8,8,256]{2,1,0:T(8,128)}, f32[1,16,8,16,128]{4,3,2,1,0:T(8,128)}) custom-call(f32[16,16,8,128]{3,2,1,0:T(8,128)} %get-tuple-element.6.c2, f32[8,3,8,128]{3,2,1,0:T(8,128)} %get-tuple-element.7.mine, f32[8,3,8,128]{3,2,1,0:T(8,128)} %get-tuple-element.8.theirs), custom_call_target="tpu_custom_call" | custom-call | tf_op jit(solution)/shard_map/pallas_call | solution.py:597

commit v3 on v2

--- a/solution.py
+++ b/solution.py
@@ -29,7 +29,7 @@
     n_row, n_col,
     flow, temp, tr, bot, sun, rates,
     c2, mine_out, theirs_out,
-    c0, c1, p0, p1, psat, fm0, fp0, fm1, fp1, fm2, kpm, kpp, kpm1, kpp1, am, ap, wmat,
+    c0, c1, p0, p1, psat, fm0, fp0, fm1, fp1, fm2, kpm, kpp, kpm1, kpp1, am, ap, wmat, whi, wlo, sbuf,
     xo, xw, xe, px_out, px_in, pf, pt, pb, ps, fr,
     send, recv, ready,
 ):
@@ -75,6 +75,15 @@
         by = by % x.shape[axis]
         return pltpu.roll(x, by, axis) if by else x
 
+    def loop(first, last, by, body):
+        def several(k, carry):
+            for r in range(by):
+                body(first + k * by + r)
+            return carry
+
+        assert (last - first) % by == 0
+        lax.fori_loop(0, (last - first) // by, several, 0)
+
     def turn_in(n, carry):
         for t in range(2):
             c0[pl.ds(2 + 8 * t, 8), n] = jnp.swapaxes(tr[0, n, :, 8 * t : 8 * t + 8, :], 0, 1)
@@ -150,7 +159,13 @@
     same = lax.rem(lax.broadcasted_iota(jnp.int32, (128, 128), 0), 8) == lax.rem(
         lax.broadcasted_iota(jnp.int32, (128, 128), 1), 8
     )
-    wmat[...] = jnp.where(same, square, 0.0)
+    whole = jnp.where(same, square, 0.0)
+    wmat[...] = whole
+    upper = whole.astype(jnp.bfloat16)
+    lower = (whole - upper.astype(jnp.float32)).astype(jnp.bfloat16)
+    for at in (0, 128):
+        whi[:, at : at + 128] = upper
+        wlo[:, at : at + 128] = lower
 
     def fill(first, field_u, field_v, field_h, field_b, field_s):
         for r in range(8):
@@ -177,7 +192,7 @@
     start(soon_n, rows_n)
     start(soon_s, rows_s)
 
-    def pack(j, carry):
+    def pack(j):
         i = j + 2
         acc = zero
         for n in range(NT):
@@ -189,9 +204,8 @@
             acc = jnp.where((lane // 2) == (8 * f + 6) // 2, roll(x, 8 * f + 6), acc)
             acc = jnp.where((lane // 2) == (8 * f + 8) // 2, roll(x, 8 * f + 10), acc)
         xo[j] = acc
-        return carry
-
-    lax.fori_loop(0, 16, pack, 0)
+
+    loop(0, 16, 2, pack)
     start(has_e, to_east)
     start(has_w, to_west)
 
@@ -209,18 +223,17 @@
             y = y + roll(y, by)
         return y
 
-    def unpack_row(j, carry):
+    def unpack_row(j):
         own, w, e = xo[j], xw[j], xe[j]
         p0[j + 2] = jnp.where(group < 2, roll(w, -4), jnp.where(group >= 6, roll(e, 4), own))
         fields = fields_of(j)
         for f in range(4):
             fp0[j + 2, f] = spread_field(fields, f)
-        return carry
 
     def fields_of(j):
         return jnp.where(group < 2, roll(xw[j], -8), jnp.where(group >= 6, xe[j], roll(xo[j], -4)))
 
-    lax.fori_loop(0, 16, unpack_row, 0)
+    loop(0, 16, 4, unpack_row)
     for side, j in ((0, 0), (1, 15)):
         px_out[side, 0] = p0[j + 2]
         px_out[side, 1] = fields_of(j)
@@ -255,12 +268,11 @@
         k[i, 1] = pressure
 
     def prepare(fm, fp, km, kp, first, last):
-        def one(i, carry):
+        def one(i):
             prepare_row(i, fm, km)
             prepare_row(i, fp, kp)
-            return carry
-
-        lax.fori_loop(first, last, one, 0)
+
+        loop(first, last, 2, one)
 
     def east_of(m, p, n=0):
         return jnp.where(lane == 127, roll(p, 121 - 8 * n), roll(m, 127))
@@ -389,33 +401,47 @@
             level < KL, jnp.exp(-above) * (1.0 - jnp.exp(-depth)), 0.0
         )
 
-    def tracer_row(i, c, p, c_new, i_new, fm_new):
+    def moved_row(i, c, p, c_new, i_new, slot):
         a = [am[i, s] for s in range(7)]
-        wet = wet_of(fm0[i, 3])
-        ghost = p[i]
-        moved = []
-        for n in range(NT):
-            x = c[i, n]
-            moved.append(
-                apply(a, x, east_of(x, ghost, n), west_of(x, ghost, n), c[i + 1, n], c[i - 1, n])
-            )
-        bent = jnp.concatenate([m * lax.rsqrt(1.0 + m * m) for m in moved], axis=0)
-        coupling = jnp.dot(
-            wmat[...], bent, precision=lax.Precision.HIGHEST, preferred_element_type=jnp.float32
-        )
-        scale = react_step * wet
-        for n in range(NT):
-            value = moved[n] + scale * coupling[8 * n : 8 * n + 8]
-            c_new[i_new, n] = value
-            if n == 0:
-                fm_new[i, 2] = fm_new[i, 2] + heat_gain * light_of(fm0[i, 3]) * wet * profile_of(
-                    value
-                )
-
-    def step1_flow(i, carry):
+        ghost = jnp.where(lane % 8 == 0, roll(p[i], -6), roll(p[i], -2))
+        lanes = pl.ds(pl.multiple_of(slot * 128, 128), 128)
+        for pair in range(NT // 2):
+            bent = []
+            for n in (2 * pair, 2 * pair + 1):
+                x = c[i, n]
+                g = roll(ghost, -8 * n)
+                x_e = roll(jnp.where(lane == 0, g, x), 127)
+                x_w = roll(jnp.where(lane == 127, g, x), 1)
+                m = apply(a, x, x_e, x_w, c[i + 1, n], c[i - 1, n])
+                c_new[i_new, n] = m
+                bent.append(m * lax.rsqrt(1.0 + m * m))
+            both = jnp.concatenate(bent, axis=0)
+            high = both.astype(jnp.bfloat16)
+            low = (both - high.astype(jnp.float32)).astype(jnp.bfloat16)
+            sbuf[16 * pair : 16 * pair + 16, lanes] = high
+            sbuf[128 + 16 * pair : 144 + 16 * pair, lanes] = low
+
+    def react_rows(rows, slot, c_new, shift, f_new):
+        part = sbuf[:, 128 * slot : 128 * slot + 256]
+        coupling = jnp.dot(whi[...], part, preferred_element_type=jnp.float32) + jnp.dot(
+            wlo[...], part, preferred_element_type=jnp.float32
+        )
+        for r, i in enumerate(rows):
+            wet = wet_of(fm0[i, 3])
+            scale = react_step * wet
+            for n in range(NT):
+                value = c_new[i - shift, n] + scale * coupling[
+                    8 * n : 8 * n + 8, 128 * r : 128 * r + 128
+                ]
+                c_new[i - shift, n] = value
+                if n == 0:
+                    f_new[i, 2] = f_new[i, 2] + heat_gain * light_of(
+                        fm0[i, 3]
+                    ) * wet * profile_of(value)
+
+    def step1_flow(i):
         flow_main(i, fm0, fp0, kpm, kpp, fm1)
         flow_packed(i)
-        return carry
 
     def packed_moved(i):
         x = p0[i]
@@ -438,30 +464,21 @@
             spread_field(value, 0)
         )
 
-    def step1_main(i, carry):
-        tracer_row(i, c0, p0, c1, i, fm1)
-        return carry
-
-    def step2_main(i, carry):
-        flow_main(i, fm1, fp1, kpm1, kpp1, fm2)
-        tracer_row(i, c1, p1, c2, i - 2, fm2)
-        return carry
-
     prepare(fm0, fp0, kpm, kpp, 2, 18)
-    lax.fori_loop(3, 17, step1_flow, 0)
-
-    def packed_in(i, carry):
+    loop(3, 17, 2, step1_flow)
+
+    def packed_in(i):
         psat[pl.ds(pl.multiple_of(8 * (i - 3), 8), 8), :] = packed_moved(i)
-        return carry
-
-    def packed_end(i, carry):
+
+    def packed_end(i):
         packed_react(i, psat[pl.ds(pl.multiple_of(8 * (i - 3), 8), 8), :])
-        return carry
-
-    lax.fori_loop(3, 17, packed_in, 0)
+
+    loop(3, 17, 7, packed_in)
     psat[...] = couple(psat[...])
-    lax.fori_loop(3, 17, packed_end, 0)
-    lax.fori_loop(3, 17, step1_main, 0)
+    loop(3, 17, 7, packed_end)
+    loop(3, 17, 1, lambda i: moved_row(i, c0, p0, c1, i, i - 3))
+    for i in range(3, 17, 2):
+        react_rows((i, i + 1), i - 3, c1, 0, fm1)
 
     @pl.when(late_s)
     def _():
@@ -470,7 +487,10 @@
             one.start()
 
     prepare(fm1, fp1, kpm1, kpp1, 3, 17)
-    lax.fori_loop(4, 16, step2_main, 0)
+    loop(4, 16, 2, lambda i: flow_main(i, fm1, fp1, kpm1, kpp1, fm2))
+    loop(4, 16, 1, lambda i: moved_row(i, c1, p1, c2, i - 2, i - 4))
+    for i in range(4, 16, 2):
+        react_rows((i, i + 1), i - 4, c2, 2, fm2)
 
     def finish(out, by, side):
         edge = out + by
@@ -484,13 +504,17 @@
         flow_packed(edge)
         flow_main(out, fm0, fp0, kpm, kpp, fm1)
         packed_react(edge, couple(packed_moved(edge)))
-        step1_main(edge, 0)
-        step1_main(out, 0)
+        moved_row(edge, c0, p0, c1, edge, 0)
+        moved_row(out, c0, p0, c1, out, 1)
+        react_rows((edge, out), 0, c1, 0, fm1)
         prepare_row(edge, fm1, kpm1)
         prepare_row(edge, fp1, kpp1)
         prepare_row(out, fm1, kpm1)
-        step2_main(edge + by, 0)
-        step2_main(edge, 0)
+        flow_main(edge + by, fm1, fp1, kpm1, kpp1, fm2)
+        flow_main(edge, fm1, fp1, kpm1, kpp1, fm2)
+        moved_row(edge + by, c1, p1, c2, edge + by - 2, 0)
+        moved_row(edge, c1, p1, c2, edge - 2, 1)
+        react_rows((edge + by, edge), 0, c2, 2, fm2)
 
     @pl.when(has_n)
     def _():
@@ -575,6 +599,9 @@
             pltpu.VMEM((20, 7) + tile, f32),
             pltpu.VMEM((20, 7) + tile, f32),
             pltpu.VMEM((128, 128), f32),
+            pltpu.VMEM((128, 256), jnp.bfloat16),
+            pltpu.VMEM((128, 256), jnp.bfloat16),
+            pltpu.VMEM((256, 14 * 128), jnp.bfloat16),
             pltpu.VMEM((16,) + tile, f32),
             pltpu.VMEM((16,) + tile, f32),
             pltpu.VMEM((16,) + tile, f32),

time: 57 us -> 49.2 us (0.86)
  the two profiles are of different devices: /device:TPU:321 before, /device:TPU:43 now
where the time goes in v3:
time: 49.2 us; the launch traced here: 49 us
  Pallas kernels  48.4 us (98%)
  between operations  0.64 us (1%)
    pallas_call x1, Pallas kernels, on_device(): pl.pallas_call(functools.partial(kernel, n_row, n_col), out_shape=(jax.Sh...  46 us
    pallas_call x1, Pallas kernels, on_device(): pl.pallas_call(lay_out, grid=(parts,), out_shape=(jax.ShapeDtypeStruct((2...  2.33 us

profile of v3, /device:TPU:43, one launch (start us, length us, event | category | flops | bytes accessed | tf_op | source)
XLA Modules:
  0.0 49.0 jit_solution(14137204949240718898)
XLA Ops:
  0.6 46.0 %shard_map.85 = (f32[16,16,8,128]{3,2,1,0:T(8,128)}, f32[8,3,8,128]{3,2,1,0:T(8,128)}, f32[8,3,8,128]{3,2,1,0:T(8,128)}) custom-call(f32[2,8,8,256]{3,2,1,0:T(8,128)} %flow.1, f32[8,8,256]{2,1,0:T(8,128)} %temp.1, f32[1,16,8,16,128]{4,3,2,1,0:T(8,128)} %tr.1, s32[8,256]{1,0:T(8,128)} %bot.1, f32[8,256]{1,0:T(8,128)} %sun.1, f32[16,16]{1,0:T(8,128)} %rates.1), custom_call_target="tpu_custom_call" | custom-call | tf_op jit(solution)/shard_map/pallas_call | solution.py:575
  46.7 2.3 %shard_map.86 = (f32[2,8,8,256]{3,2,1,0:T(8,128)}, f32[8,8,256]{2,1,0:T(8,128)}, f32[1,16,8,16,128]{4,3,2,1,0:T(8,128)}) custom-call(f32[16,16,8,128]{3,2,1,0:T(8,128)} %get-tuple-element.6.c2, f32[8,3,8,128]{3,2,1,0:T(8,128)} %get-tuple-element.7.mine, f32[8,3,8,128]{3,2,1,0:T(8,128)} %get-tuple-element.8.theirs), custom_call_target="tpu_custom_call" | custom-call | tf_op jit(solution)/shard_map/pallas_call | solution.py:624

commit v4 on v3

--- a/solution.py
+++ b/solution.py
@@ -30,7 +30,7 @@
     flow, temp, tr, bot, sun, rates,
     c2, mine_out, theirs_out,
     c0, c1, p0, p1, psat, fm0, fp0, fm1, fp1, fm2, kpm, kpp, kpm1, kpp1, am, ap, wmat, whi, wlo, sbuf,
-    xo, xw, xe, px_out, px_in, pf, pt, pb, ps, fr,
+    xo, xf, te, tw, xw, xe, px_out, px_in, pf, pt, pb, ps, fr,
     send, recv, ready,
 ):
     row = lax.axis_index("row")
@@ -105,8 +105,8 @@
         copy(bot.at[:, other_half], pb, 2, partner),
         copy(sun.at[:, other_half], ps, 3, partner),
     )
-    to_east = copy(xo, xw, 4, east)
-    to_west = copy(xo, xe, 5, west)
+    to_east = copy(te, xw, 4, east)
+    to_west = copy(tw, xe, 5, west)
     near_n = copy(c0.at[17], c0.at[1], 6, north)
     near_s = copy(c0.at[2], c0.at[18], 7, south)
     far_n = copy(c0.at[16], c0.at[0], 8, north)
@@ -124,7 +124,7 @@
 
     for here, ref, at, length in (
         (has_s, c0, 0, 2), (has_n, c0, 18, 2), (has_s, fm0, 0, 2), (has_n, fm0, 18, 2),
-        (has_w, xw, 0, 16), (has_e, xe, 0, 16), (has_s, px_in, 0, 1), (has_n, px_in, 1, 1),
+        (has_w, xw, 0, 5), (has_e, xe, 0, 5), (has_s, px_in, 0, 1), (has_n, px_in, 1, 1),
     ):
         @pl.when(jnp.logical_not(here))
         def _(ref=ref, at=at, length=length):
@@ -142,8 +142,8 @@
         def _(target=target, k=k):
             pl.semaphore_signal(ready.at[k], inc=1, device_id=target, device_id_type=MESH)
 
-    start(soon_n, near_n, far_n)
-    start(soon_s, near_s, far_s)
+    start(soon_n, near_n)
+    start(soon_s, near_s)
 
     spread = (
         lax.broadcasted_iota(jnp.int32, (128, NT), 0) // 8
@@ -189,8 +189,6 @@
     for one in to_partner:
         one.wait_recv()
     fill(10 - 8 * half, turn(pf[0]), turn(pf[1]), turn(pt[...]), pb[...], ps[...])
-    start(soon_n, rows_n)
-    start(soon_s, rows_s)
 
     def pack(j):
         i = j + 2
@@ -199,15 +197,32 @@
             x = c0[i, n]
             acc = jnp.where((lane // 2) == (8 * n + 2) // 2, roll(x, 8 * n + 2), acc)
             acc = jnp.where((lane // 2) == (8 * n + 4) // 2, roll(x, 8 * n + 6), acc)
+        xo[j] = acc
+        acc = zero
         for f in range(4):
             x = fm0[i, f]
-            acc = jnp.where((lane // 2) == (8 * f + 6) // 2, roll(x, 8 * f + 6), acc)
-            acc = jnp.where((lane // 2) == (8 * f + 8) // 2, roll(x, 8 * f + 10), acc)
-        xo[j] = acc
+            acc = jnp.where((lane // 2) == (8 * f + 2) // 2, roll(x, 8 * f + 2), acc)
+            acc = jnp.where((lane // 2) == (8 * f + 4) // 2, roll(x, 8 * f + 6), acc)
+        xf[j] = acc
 
     loop(0, 16, 2, pack)
+
+    for tile_of, first in ((te, 4), (tw, 2)):
+        fields = zero
+        for q in range(4):
+            tracers = zero
+            for r in range(4):
+                here = group // 2 == r
+                tracers = jnp.where(here, roll(xo[4 * q + r], 2 * r - first), tracers)
+                fields = jnp.where(
+                    here & (lane // 32 == q), roll(xf[4 * q + r], 32 * q + 2 * r - first), fields
+                )
+            tile_of[q] = tracers
+        tile_of[4] = fields
     start(has_e, to_east)
     start(has_w, to_west)
+    start(soon_n, rows_n)
+    start(soon_s, rows_s)
 
     @pl.when(has_w)
     def _():
@@ -223,27 +238,29 @@
             y = y + roll(y, by)
         return y
 
-    def unpack_row(j):
-        own, w, e = xo[j], xw[j], xe[j]
-        p0[j + 2] = jnp.where(group < 2, roll(w, -4), jnp.where(group >= 6, roll(e, 4), own))
+    def sides(own, w, e, by_w, by_e):
+        return jnp.where(group < 2, roll(w, by_w), jnp.where(group >= 6, roll(e, by_e), own))
+
+    def fields_of(j):
+        by = 32 * (j // 4) + 2 * (j % 4)
+        return sides(xf[j], xw[4], xe[4], -by, 6 - by)
+
+    for j in range(16):
+        q, by = j // 4, 2 * (j % 4)
+        p0[j + 2] = sides(xo[j], xw[q], xe[q], -by, 6 - by)
         fields = fields_of(j)
         for f in range(4):
             fp0[j + 2, f] = spread_field(fields, f)
-
-    def fields_of(j):
-        return jnp.where(group < 2, roll(xw[j], -8), jnp.where(group >= 6, xe[j], roll(xo[j], -4)))
-
-    loop(0, 16, 4, unpack_row)
     for side, j in ((0, 0), (1, 15)):
         px_out[side, 0] = p0[j + 2]
         px_out[side, 1] = fields_of(j)
-    start(soon_n, edge_n)
-    start(soon_s, edge_s)
+    start(soon_n, edge_n, far_n)
+    start(soon_s, edge_s, far_s)
 
     @pl.when(late_n)
     def _():
         pl.semaphore_wait(ready.at[0], 1)
-        for one in (near_n, rows_n, far_n, edge_n):
+        for one in (near_n, rows_n, edge_n, far_n):
             one.start()
 
     def wet_of(aux):
@@ -483,7 +500,7 @@
     @pl.when(late_s)
     def _():
         pl.semaphore_wait(ready.at[1], 1)
-        for one in (near_s, rows_s, far_s, edge_s):
+        for one in (near_s, rows_s, edge_s, far_s):
             one.start()
 
     prepare(fm1, fp1, kpm1, kpp1, 3, 17)
@@ -604,7 +621,10 @@
             pltpu.VMEM((256, 14 * 128), jnp.bfloat16),
             pltpu.VMEM((16,) + tile, f32),
             pltpu.VMEM((16,) + tile, f32),
-            pltpu.VMEM((16,) + tile, f32),
+            pltpu.VMEM((5,) + tile, f32),
+            pltpu.VMEM((5,) + tile, f32),
+            pltpu.VMEM((5,) + tile, f32),
+            pltpu.VMEM((5,) + tile, f32),
             pltpu.VMEM((2, 2) + tile, f32),
             pltpu.VMEM((2, 2) + tile, f32),
             pltpu.VMEM((2, NZ, 8, 128), f32),

time: 49.2 us -> 47.6 us (0.967)
  Pallas kernels: 48.4 us -> 46.8 us
    pallas_call x1, Pallas kernels: 46 us -> 44.5 us  [on_device(): pl.pallas_call(functools.partial(kernel, n_row, n_col), out_shape=(jax.Sh...]
where the time goes in v4:
time: 47.6 us; the launch traced here: 47.4 us
  Pallas kernels  46.8 us (98%)
  between operations  0.64 us (1%)
    pallas_call x1, Pallas kernels, on_device(): pl.pallas_call(functools.partial(kernel, n_row, n_col), out_shape=(jax.Sh...  44.5 us
    pallas_call x1, Pallas kernels, on_device(): pl.pallas_call(lay_out, grid=(parts,), out_shape=(jax.ShapeDtypeStruct((2...  2.33 us

profile of v4, /device:TPU:43, one launch (start us, length us, event | category | flops | bytes accessed | tf_op | source)
XLA Modules:
  0.0 47.4 jit_solution(13129506216950829518)
XLA Ops:
  0.6 44.5 %shard_map.85 = (f32[16,16,8,128]{3,2,1,0:T(8,128)}, f32[8,3,8,128]{3,2,1,0:T(8,128)}, f32[8,3,8,128]{3,2,1,0:T(8,128)}) custom-call(f32[2,8,8,256]{3,2,1,0:T(8,128)} %flow.1, f32[8,8,256]{2,1,0:T(8,128)} %temp.1, f32[1,16,8,16,128]{4,3,2,1,0:T(8,128)} %tr.1, s32[8,256]{1,0:T(8,128)} %bot.1, f32[8,256]{1,0:T(8,128)} %sun.1, f32[16,16]{1,0:T(8,128)} %rates.1), custom_call_target="tpu_custom_call" | custom-call | tf_op jit(solution)/shard_map/pallas_call | solution.py:592
  45.1 2.3 %shard_map.86 = (f32[2,8,8,256]{3,2,1,0:T(8,128)}, f32[8,8,256]{2,1,0:T(8,128)}, f32[1,16,8,16,128]{4,3,2,1,0:T(8,128)}) custom-call(f32[16,16,8,128]{3,2,1,0:T(8,128)} %get-tuple-element.6.c2, f32[8,3,8,128]{3,2,1,0:T(8,128)} %get-tuple-element.7.mine, f32[8,3,8,128]{3,2,1,0:T(8,128)} %get-tuple-element.8.theirs), custom_call_target="tpu_custom_call" | custom-call | tf_op jit(solution)/shard_map/pallas_call | solution.py:644

commit v5 on v4

--- a/solution.py
+++ b/solution.py
@@ -27,12 +27,22 @@
 
 def kernel(
     n_row, n_col,
-    flow, temp, tr, bot, sun, rates,
+    flow_h, temp_h, tr_h, bot_h, sun_h, rates_h,
     c2, mine_out, theirs_out,
     c0, c1, p0, p1, psat, fm0, fp0, fm1, fp1, fm2, kpm, kpp, kpm1, kpp1, am, ap, wmat, whi, wlo, sbuf,
     xo, xf, te, tw, xw, xe, px_out, px_in, pf, pt, pb, ps, fr,
-    send, recv, ready,
+    flow, temp, tr, bot, sun, rates,
+    send, recv, ready, load,
 ):
+    loads = [
+        pltpu.make_async_copy(src, dst, load.at[k])
+        for k, (src, dst) in enumerate(
+            ((tr_h, tr), (flow_h, flow), (temp_h, temp), (bot_h, bot), (sun_h, sun), (rates_h, rates))
+        )
+    ]
+    for one in loads:
+        one.start()
+
     row = lax.axis_index("row")
     col = lax.axis_index("col")
     half = lax.rem(row, 2)
@@ -89,7 +99,10 @@
             c0[pl.ds(2 + 8 * t, 8), n] = jnp.swapaxes(tr[0, n, :, 8 * t : 8 * t + 8, :], 0, 1)
         return carry
 
+    loads[0].wait()
     lax.fori_loop(0, NT, turn_in, 0)
+    for one in loads[1:]:
+        one.wait()
 
     def copy(src, dst, k, target):
         return pltpu.make_async_remote_copy(
@@ -142,7 +155,7 @@
         def _(target=target, k=k):
             pl.semaphore_signal(ready.at[k], inc=1, device_id=target, device_id_type=MESH)
 
-    start(soon_n, near_n)
+    start(soon_n, near_n, far_n)
     start(soon_s, near_s)
 
     spread = (
@@ -254,7 +267,7 @@
     for side, j in ((0, 0), (1, 15)):
         px_out[side, 0] = p0[j + 2]
         px_out[side, 1] = fields_of(j)
-    start(soon_n, edge_n, far_n)
+    start(soon_n, edge_n)
     start(soon_s, edge_s, far_s)
 
     @pl.when(late_n)
@@ -298,9 +311,8 @@
         return jnp.where(lane == 0, roll(p, 127 - 8 * n), roll(m, 1))
 
     def apply(a, x, xe_, xw_, xn, xs):
-        return (
-            a[0] * x + a[1] * xe_ + a[2] * xw_ + a[3] * xn + a[4] * xs
-            + a[5] * roll(x, 1, 0) + a[6] * roll(x, 7, 0)
+        return ((a[0] * x + a[3] * xn) + (a[4] * xs + a[5] * roll(x, 1, 0))) + (
+            a[6] * roll(x, 7, 0) + (a[1] * xe_ + a[2] * xw_)
         )
 
     def flow_row(i, f, k, aux, e_of, w_of, coriolis):
@@ -493,7 +505,7 @@
     loop(3, 17, 7, packed_in)
     psat[...] = couple(psat[...])
     loop(3, 17, 7, packed_end)
-    loop(3, 17, 1, lambda i: moved_row(i, c0, p0, c1, i, i - 3))
+    loop(3, 17, 2, lambda i: moved_row(i, c0, p0, c1, i, i - 3))
     for i in range(3, 17, 2):
         react_rows((i, i + 1), i - 3, c1, 0, fm1)
 
@@ -505,7 +517,7 @@
 
     prepare(fm1, fp1, kpm1, kpp1, 3, 17)
     loop(4, 16, 2, lambda i: flow_main(i, fm1, fp1, kpm1, kpp1, fm2))
-    loop(4, 16, 1, lambda i: moved_row(i, c1, p1, c2, i - 2, i - 4))
+    loop(4, 16, 2, lambda i: moved_row(i, c1, p1, c2, i - 2, i - 4))
     for i in range(4, 16, 2):
         react_rows((i, i + 1), i - 4, c2, 2, fm2)
 
@@ -596,7 +608,7 @@
             jax.ShapeDtypeStruct((8, 3) + tile, f32),
             jax.ShapeDtypeStruct((8, 3) + tile, f32),
         ),
-        in_specs=[vmem] * 6,
+        in_specs=[pl.BlockSpec(memory_space=pl.ANY)] * 6,
         out_specs=(vmem, vmem, vmem),
         scratch_shapes=[
             pltpu.VMEM((20, NT) + tile, f32),
@@ -632,9 +644,16 @@
             pltpu.VMEM((8, 128), jnp.int32),
             pltpu.VMEM((8, 128), f32),
             pltpu.VMEM((8, 3) + tile, f32),
+            pltpu.VMEM((2, NZ, 8, 256), f32),
+            pltpu.VMEM((NZ, 8, 256), f32),
+            pltpu.VMEM((1, NT, NZ, 16, 128), f32),
+            pltpu.VMEM((8, 256), jnp.int32),
+            pltpu.VMEM((8, 256), f32),
+            pltpu.VMEM((NT, NT), f32),
             pltpu.SemaphoreType.DMA((15,)),
             pltpu.SemaphoreType.DMA((15,)),
             pltpu.SemaphoreType.REGULAR((2,)),
+            pltpu.SemaphoreType.DMA((6,)),
         ],
         compiler_params=pltpu.CompilerParams(collective_id=0, has_side_effects=True),
     )(*args)

time: 47.6 us -> 43.3 us (0.910)
  the two profiles are of different devices: /device:TPU:43 before, /device:TPU:61 now
where the time goes in v5:
time: 43.3 us; the launch traced here: 43.1 us
  Pallas kernels  42.5 us (98%)
  between operations  0.64 us (1%)
    pallas_call x1, Pallas kernels, on_device(): pl.pallas_call(functools.partial(kernel, n_row, n_col), out_shape=(jax.Sh...  40.2 us
    pallas_call x1, Pallas kernels, on_device(): pl.pallas_call(lay_out, grid=(parts,), out_shape=(jax.ShapeDtypeStruct((2...  2.33 us

profile of v5, /device:TPU:61, one launch (start us, length us, event | category | flops | bytes accessed | tf_op | source)
XLA Modules:
  0.0 43.1 jit_solution(8021154547369152946)
XLA Ops:
  0.6 40.2 %shard_map.85 = (f32[16,16,8,128]{3,2,1,0:T(8,128)}, f32[8,3,8,128]{3,2,1,0:T(8,128)}, f32[8,3,8,128]{3,2,1,0:T(8,128)}) custom-call(f32[2,8,8,256]{3,2,1,0:T(8,128)} %flow_h.1, f32[8,8,256]{2,1,0:T(8,128)} %temp_h.1, f32[1,16,8,16,128]{4,3,2,1,0:T(8,128)} %tr_h.1, s32[8,256]{1,0:T(8,128)} %bot_h.1, f32[8,256]{1,0:T(8,128)} %sun_h.1, f32[16,16]{1,0:T(8,128)} %rates_h.1), custom_call_target="tpu_custom_call" | custom-call | tf_op jit(solution)/shard_map/pallas_call | solution.py:604
  40.8 2.3 %shard_map.86 = (f32[2,8,8,256]{3,2,1,0:T(8,128)}, f32[8,8,256]{2,1,0:T(8,128)}, f32[1,16,8,16,128]{4,3,2,1,0:T(8,128)}) custom-call(f32[16,16,8,128]{3,2,1,0:T(8,128)} %get-tuple-element.6.c2, f32[8,3,8,128]{3,2,1,0:T(8,128)} %get-tuple-element.7.mine, f32[8,3,8,128]{3,2,1,0:T(8,128)} %get-tuple-element.8.theirs), custom_call_target="tpu_custom_call" | custom-call | tf_op jit(solution)/shard_map/pallas_call | solution.py:663

commit v6 on v5

--- a/solution.py
+++ b/solution.py
@@ -12,6 +12,7 @@
 NZ = 8
 KL = 4
 PERIOD = 4
+RUN = 4
 
 time_step = 0.2
 viscosity = 0.2
@@ -64,6 +65,7 @@
     late_s = has_s & (place == 0)
     soon_n = has_n & (place == PERIOD - 1)
     soon_s = has_s & (place != 0)
+    farthest = lax.rem(col, RUN) == 0
 
     barrier = pltpu.get_barrier_semaphore()
     for tells, target in ((has_e, east), (has_w, west), (late_n, north), (late_s, south)):
@@ -124,8 +126,8 @@
     near_s = copy(c0.at[2], c0.at[18], 7, south)
     far_n = copy(c0.at[16], c0.at[0], 8, north)
     far_s = copy(c0.at[3], c0.at[19], 9, south)
-    rows_n = copy(fm0.at[pl.ds(16, 2)], fm0.at[pl.ds(0, 2)], 10, north)
-    rows_s = copy(fm0.at[pl.ds(2, 2)], fm0.at[pl.ds(18, 2)], 11, south)
+    rows_n = copy(fm0.at[pl.ds(16, 2), pl.ds(0, 3)], fm0.at[pl.ds(0, 2), pl.ds(0, 3)], 10, north)
+    rows_s = copy(fm0.at[pl.ds(2, 2), pl.ds(0, 3)], fm0.at[pl.ds(18, 2), pl.ds(0, 3)], 11, south)
     edge_n = copy(px_out.at[1], px_in.at[0], 12, north)
     edge_s = copy(px_out.at[0], px_in.at[1], 13, south)
 
@@ -155,7 +157,8 @@
         def _(target=target, k=k):
             pl.semaphore_signal(ready.at[k], inc=1, device_id=target, device_id_type=MESH)
 
-    start(soon_n, near_n, far_n)
+    start(soon_n, near_n)
+    start(soon_n & farthest, far_n)
     start(soon_s, near_s)
 
     spread = (
@@ -264,10 +267,14 @@
         fields = fields_of(j)
         for f in range(4):
             fp0[j + 2, f] = spread_field(fields, f)
-    for side, j in ((0, 0), (1, 15)):
-        px_out[side, 0] = p0[j + 2]
-        px_out[side, 1] = fields_of(j)
+    for side, j, two in ((0, 0, (2, 3)), (1, 15, (16, 17))):
+        px_out[side, 0] = jnp.where(
+            (group == 1) | (group == 6), p0[j + 2], roll(fields_of(j), 1)
+        )
+        px_out[side, 1] = jnp.where(level < 2, fm0[two[0], 3], roll(fm0[two[1], 3], 2, 0))
+
     start(soon_n, edge_n)
+    start(soon_n & jnp.logical_not(farthest), far_n)
     start(soon_s, edge_s, far_s)
 
     @pl.when(late_n)
@@ -525,7 +532,10 @@
         edge = out + by
         p0[out] = px_in[side, 0]
         for f in range(4):
-            fp0[out, f] = spread_field(px_in[side, 1], f)
+            fp0[out, f] = spread_field(roll(px_in[side, 0], -1), f)
+        low = min(out, out - by)
+        fm0[low, 3] = px_in[side, 1]
+        fm0[low + 1, 3] = roll(px_in[side, 1], -2, 0)
         prepare_row(out - by, fm0, kpm)
         prepare_row(out, fm0, kpm)
         prepare_row(out, fp0, kpp)
@@ -658,7 +668,7 @@
         compiler_params=pltpu.CompilerParams(collective_id=0, has_side_effects=True),
     )(*args)
     small = pl.BlockSpec((8, 3) + tile, lambda g: (0, 0, 0, 0))
-    parts = 2
+    parts = 4
     return tuple(
         pl.pallas_call(
             lay_out,

time: 43.3 us -> 46.1 us (1.065)
  the two profiles are of different devices: /device:TPU:61 before, /device:TPU:53 now
where the time goes in v6:
time: 46.1 us; the launch traced here: 45.9 us
  Pallas kernels  45.3 us (98%)
  between operations  0.64 us (1%)
    pallas_call x1, Pallas kernels, on_device(): pl.pallas_call(functools.partial(kernel, n_row, n_col), out_shape=(jax.Sh...  41.6 us
    pallas_call x1, Pallas kernels, on_device(): pl.pallas_call(lay_out, grid=(parts,), out_shape=(jax.ShapeDtypeStruct((2...  3.66 us

profile of v6, /device:TPU:53, one launch (start us, length us, event | category | flops | bytes accessed | tf_op | source)
XLA Modules:
  0.0 45.9 jit_solution(6668215110262191511)
XLA Ops:
  0.6 41.6 %shard_map.85 = (f32[16,16,8,128]{3,2,1,0:T(8,128)}, f32[8,3,8,128]{3,2,1,0:T(8,128)}, f32[8,3,8,128]{3,2,1,0:T(8,128)}) custom-call(f32[2,8,8,256]{3,2,1,0:T(8,128)} %flow_h.1, f32[8,8,256]{2,1,0:T(8,128)} %temp_h.1, f32[1,16,8,16,128]{4,3,2,1,0:T(8,128)} %tr_h.1, s32[8,256]{1,0:T(8,128)} %bot_h.1, f32[8,256]{1,0:T(8,128)} %sun_h.1, f32[16,16]{1,0:T(8,128)} %rates_h.1), custom_call_target="tpu_custom_call" | custom-call | tf_op jit(solution)/shard_map/pallas_call | solution.py:614
  42.2 3.7 %shard_map.86 = (f32[2,8,8,256]{3,2,1,0:T(8,128)}, f32[8,8,256]{2,1,0:T(8,128)}, f32[1,16,8,16,128]{4,3,2,1,0:T(8,128)}) custom-call(f32[16,16,8,128]{3,2,1,0:T(8,128)} %get-tuple-element.6.c2, f32[8,3,8,128]{3,2,1,0:T(8,128)} %get-tuple-element.7.mine, f32[8,3,8,128]{3,2,1,0:T(8,128)} %get-tuple-element.8.theirs), custom_call_target="tpu_custom_call" | custom-call | tf_op jit(solution)/shard_map/pallas_call | solution.py:673

commit v7 on v5

--- a/solution.py
+++ b/solution.py
@@ -155,7 +155,7 @@
         def _(target=target, k=k):
             pl.semaphore_signal(ready.at[k], inc=1, device_id=target, device_id_type=MESH)
 
-    start(soon_n, near_n, far_n)
+    start(soon_n, near_n)
     start(soon_s, near_s)
 
     spread = (
@@ -234,7 +234,7 @@
         tile_of[4] = fields
     start(has_e, to_east)
     start(has_w, to_west)
-    start(soon_n, rows_n)
+    start(soon_n, rows_n, far_n)
     start(soon_s, rows_s)
 
     @pl.when(has_w)
@@ -451,7 +451,7 @@
             sbuf[128 + 16 * pair : 144 + 16 * pair, lanes] = low
 
     def react_rows(rows, slot, c_new, shift, f_new):
-        part = sbuf[:, 128 * slot : 128 * slot + 256]
+        part = sbuf[:, 128 * slot : 128 * (slot + len(rows))]
         coupling = jnp.dot(whi[...], part, preferred_element_type=jnp.float32) + jnp.dot(
             wlo[...], part, preferred_element_type=jnp.float32
         )
@@ -521,43 +521,49 @@
     for i in range(4, 16, 2):
         react_rows((i, i + 1), i - 4, c2, 2, fm2)
 
-    def finish(out, by, side):
+    def finish_near(out, by):
+        edge = out + by
+        prepare_row(out, fm0, kpm)
+        flow_main(edge, fm0, fp0, kpm, kpp, fm1)
+        moved_row(edge, c0, p0, c1, edge, 0)
+        react_rows((edge,), 0, c1, 0, fm1)
+        prepare_row(edge, fm1, kpm1)
+        flow_main(edge + by, fm1, fp1, kpm1, kpp1, fm2)
+        moved_row(edge + by, c1, p1, c2, edge + by - 2, 1)
+        react_rows((edge + by,), 1, c2, 2, fm2)
+
+    def finish_far(out, by, side):
         edge = out + by
         p0[out] = px_in[side, 0]
         for f in range(4):
             fp0[out, f] = spread_field(px_in[side, 1], f)
         prepare_row(out - by, fm0, kpm)
-        prepare_row(out, fm0, kpm)
         prepare_row(out, fp0, kpp)
-        flow_main(edge, fm0, fp0, kpm, kpp, fm1)
         flow_packed(edge)
         flow_main(out, fm0, fp0, kpm, kpp, fm1)
         packed_react(edge, couple(packed_moved(edge)))
-        moved_row(edge, c0, p0, c1, edge, 0)
-        moved_row(out, c0, p0, c1, out, 1)
-        react_rows((edge, out), 0, c1, 0, fm1)
-        prepare_row(edge, fm1, kpm1)
+        moved_row(out, c0, p0, c1, out, 2)
+        react_rows((out,), 2, c1, 0, fm1)
         prepare_row(edge, fp1, kpp1)
         prepare_row(out, fm1, kpm1)
-        flow_main(edge + by, fm1, fp1, kpm1, kpp1, fm2)
         flow_main(edge, fm1, fp1, kpm1, kpp1, fm2)
-        moved_row(edge + by, c1, p1, c2, edge + by - 2, 0)
-        moved_row(edge, c1, p1, c2, edge - 2, 1)
-        react_rows((edge + by, edge), 0, c2, 2, fm2)
-
-    @pl.when(has_n)
-    def _():
-        for one in (near_s, far_s, rows_s, edge_s):
-            one.wait_recv()
-
-    finish(18, -1, 1)
-
-    @pl.when(has_s)
-    def _():
-        for one in (near_n, far_n, rows_n, edge_n):
-            one.wait_recv()
-
-    finish(1, 1, 0)
+        moved_row(edge, c1, p1, c2, edge - 2, 3)
+        react_rows((edge,), 3, c2, 2, fm2)
+
+    def arrive(here, *copies):
+        @pl.when(here)
+        def _():
+            for one in copies:
+                one.wait_recv()
+
+    arrive(has_n, near_s, rows_s)
+    finish_near(18, -1)
+    arrive(has_n, far_s, edge_s)
+    finish_far(18, -1, 1)
+    arrive(has_s, near_n, rows_n)
+    finish_near(1, 1)
+    arrive(has_s, far_n, edge_n)
+    finish_far(1, 1, 0)
 
     back = copy(fm2.at[pl.ds(10 - 8 * half, 8)], fr, 14, partner)
     back.start()
@@ -658,7 +664,7 @@
         compiler_params=pltpu.CompilerParams(collective_id=0, has_side_effects=True),
     )(*args)
     small = pl.BlockSpec((8, 3) + tile, lambda g: (0, 0, 0, 0))
-    parts = 2
+    parts = 1
     return tuple(
         pl.pallas_call(
             lay_out,

time: 43.3 us -> 44.8 us (1.035)
  the two profiles are of different devices: /device:TPU:61 before, /device:TPU:47 now
where the time goes in v7:
time: 44.8 us; the launch traced here: 44.6 us
  Pallas kernels  43.9 us (98%)
  between operations  0.64 us (1%)
    pallas_call x1, Pallas kernels, on_device(): pl.pallas_call(functools.partial(kernel, n_row, n_col), out_shape=(jax.Sh...  41.3 us
    pallas_call x1, Pallas kernels, on_device(): pl.pallas_call(lay_out, grid=(parts,), out_shape=(jax.ShapeDtypeStruct((2...  2.63 us

profile of v7, /device:TPU:47, one launch (start us, length us, event | category | flops | bytes accessed | tf_op | source)
XLA Modules:
  0.0 44.6 jit_solution(7226725561649297952)
XLA Ops:
  0.6 41.3 %shard_map.85 = (f32[16,16,8,128]{3,2,1,0:T(8,128)}, f32[8,3,8,128]{3,2,1,0:T(8,128)}, f32[8,3,8,128]{3,2,1,0:T(8,128)}) custom-call(f32[2,8,8,256]{3,2,1,0:T(8,128)} %flow_h.1, f32[8,8,256]{2,1,0:T(8,128)} %temp_h.1, f32[1,16,8,16,128]{4,3,2,1,0:T(8,128)} %tr_h.1, s32[8,256]{1,0:T(8,128)} %bot_h.1, f32[8,256]{1,0:T(8,128)} %sun_h.1, f32[16,16]{1,0:T(8,128)} %rates_h.1), custom_call_target="tpu_custom_call" | custom-call | tf_op jit(solution)/shard_map/pallas_call | solution.py:610
  41.9 2.6 %shard_map.86 = (f32[2,8,8,256]{3,2,1,0:T(8,128)}, f32[8,8,256]{2,1,0:T(8,128)}, f32[1,16,8,16,128]{4,3,2,1,0:T(8,128)}) custom-call(f32[16,16,8,128]{3,2,1,0:T(8,128)} %get-tuple-element.6.c2, f32[8,3,8,128]{3,2,1,0:T(8,128)} %get-tuple-element.7.mine, f32[8,3,8,128]{3,2,1,0:T(8,128)} %get-tuple-element.8.theirs), custom_call_target="tpu_custom_call" | custom-call | tf_op jit(solution)/shard_map/pallas_call | solution.py:669

commit v8 on v5

--- a/solution.py
+++ b/solution.py
@@ -12,6 +12,7 @@
 NZ = 8
 KL = 4
 PERIOD = 4
+RUN = 4
 
 time_step = 0.2
 viscosity = 0.2
@@ -64,15 +65,19 @@
     late_s = has_s & (place == 0)
     soon_n = has_n & (place == PERIOD - 1)
     soon_s = has_s & (place != 0)
+    wrap_w = has_w & (half == 0) & (lax.rem(col, RUN) == 0)
+    wrap_e = has_e & (half == 1) & (lax.rem(col, RUN) == RUN - 1)
 
     barrier = pltpu.get_barrier_semaphore()
-    for tells, target in ((has_e, east), (has_w, west), (late_n, north), (late_s, south)):
+    for tells, target in (
+        (has_e & jnp.logical_not(wrap_e), east), (has_w, west), (late_n, north), (late_s, south)
+    ):
         @pl.when(tells)
         def _(target=target):
             pl.semaphore_signal(barrier, inc=1, device_id=target, device_id_type=MESH)
 
     count = jnp.int32(0)
-    for waits in (has_e, has_w, soon_n, soon_s):
+    for waits in (has_e, has_w & jnp.logical_not(wrap_w), soon_n, soon_s):
         count = count + waits.astype(jnp.int32)
 
     lane = lax.broadcasted_iota(jnp.int32, (NZ, 128), 1)
@@ -150,7 +155,7 @@
     pl.semaphore_wait(barrier, count)
     for one in to_partner:
         one.start()
-    for here, target, k in ((soon_s, south, 0), (soon_n, north, 1)):
+    for here, target, k in ((soon_s, south, 0), (soon_n, north, 1), (wrap_e, east, 2)):
         @pl.when(here)
         def _(target=target, k=k):
             pl.semaphore_signal(ready.at[k], inc=1, device_id=target, device_id_type=MESH)
@@ -233,6 +238,11 @@
             tile_of[q] = tracers
         tile_of[4] = fields
     start(has_e, to_east)
+
+    @pl.when(wrap_w)
+    def _():
+        pl.semaphore_wait(ready.at[2], 1)
+
     start(has_w, to_west)
     start(soon_n, rows_n)
     start(soon_s, rows_s)
@@ -652,7 +662,7 @@
             pltpu.VMEM((NT, NT), f32),
             pltpu.SemaphoreType.DMA((15,)),
             pltpu.SemaphoreType.DMA((15,)),
-            pltpu.SemaphoreType.REGULAR((2,)),
+            pltpu.SemaphoreType.REGULAR((3,)),
             pltpu.SemaphoreType.DMA((6,)),
         ],
         compiler_params=pltpu.CompilerParams(collective_id=0, has_side_effects=True),

time: 43.3 us -> 43.3 us (level)
  the two profiles are of different devices: /device:TPU:61 before, /device:TPU:183 now
where the time goes in v8:
time: 43.3 us; the launch traced here: 43.1 us
  Pallas kernels  42.5 us (98%)
  between operations  0.64 us (1%)
    pallas_call x1, Pallas kernels, on_device(): pl.pallas_call(functools.partial(kernel, n_row, n_col), out_shape=(jax.Sh...  40.1 us
    pallas_call x1, Pallas kernels, on_device(): pl.pallas_call(lay_out, grid=(parts,), out_shape=(jax.ShapeDtypeStruct((2...  2.33 us

profile of v8, /device:TPU:183, one launch (start us, length us, event | category | flops | bytes accessed | tf_op | source)
XLA Modules:
  0.0 43.1 jit_solution(15343274959237857265)
XLA Ops:
  0.6 40.1 %shard_map.85 = (f32[16,16,8,128]{3,2,1,0:T(8,128)}, f32[8,3,8,128]{3,2,1,0:T(8,128)}, f32[8,3,8,128]{3,2,1,0:T(8,128)}) custom-call(f32[2,8,8,256]{3,2,1,0:T(8,128)} %flow_h.1, f32[8,8,256]{2,1,0:T(8,128)} %temp_h.1, f32[1,16,8,16,128]{4,3,2,1,0:T(8,128)} %tr_h.1, s32[8,256]{1,0:T(8,128)} %bot_h.1, f32[8,256]{1,0:T(8,128)} %sun_h.1, f32[16,16]{1,0:T(8,128)} %rates_h.1), custom_call_target="tpu_custom_call" | custom-call | tf_op jit(solution)/shard_map/pallas_call | solution.py:614
  40.8 2.3 %shard_map.86 = (f32[2,8,8,256]{3,2,1,0:T(8,128)}, f32[8,8,256]{2,1,0:T(8,128)}, f32[1,16,8,16,128]{4,3,2,1,0:T(8,128)}) custom-call(f32[16,16,8,128]{3,2,1,0:T(8,128)} %get-tuple-element.6.c2, f32[8,3,8,128]{3,2,1,0:T(8,128)} %get-tuple-element.7.mine, f32[8,3,8,128]{3,2,1,0:T(8,128)} %get-tuple-element.8.theirs), custom_call_target="tpu_custom_call" | custom-call | tf_op jit(solution)/shard_map/pallas_call | solution.py:673
